TPU v7x, 32 devices: a whole 2x2x4 slice. The times are simulated.
32 devices in a mesh: gx: 2 (over x), gy: 4 (over z), gz: 4 (over y, core).
Axes of the slice: x: 2, y: 2, z: 4, core: 2. Of those that a mesh axis runs over, the one named last changes fastest.
Arguments:
- volume: float32 [16, 8, 64, 512], P(None, 'gx', 'gy', 'gz'), may hold values from -26 to 26
- weight: float32 [16, 16, 3, 3, 3], replicated, may hold values from -0.3125 to 0.3125
- gamma: float32 [16], replicated, may hold values from 0.5 to 1.5
- beta: float32 [16], replicated, may hold values from -0.5 to 0.5
- cotangent: float32 [16, 8, 64, 512], P(None, 'gx', 'gy', 'gz'), may hold values from -6 to 6
Outputs:
- input_grad: float32 [16, 8, 64, 512], P(None, 'gx', 'gy', 'gz')
- weight_grad: float32 [16, 16, 3, 3, 3], replicated
- gamma_grad: float32 [16], replicated
- beta_grad: float32 [16], replicated
All inputs are finite; a program needn't handle non-finite values.
Results may differ from a plain program's by a relative error of at most 0.0003.
Values sent between devices are 32-bit elements; how exact they have to be, the bound alone decides.
No kernel may reach another device: no remote copies, remote signals or barrier semaphores. Data moves between devices by JAX's collectives and lax.ppermute only.
A program may use at most 64 MiB of HBM per device.

v0:
```python
import jax
import jax.numpy as jnp
from jax import lax
from jax.sharding import PartitionSpec as P


def with_halo(block, sides, width):
    for axis, dim in sides:
        count = lax.axis_size(axis)
        forward = [(i, i + 1) for i in range(count - 1)]
        forward.append((count - 1, 0))
        backward = [(target, source) for source, target in forward]
        low = lax.ppermute(
            lax.slice_in_dim(block, block.shape[dim] - width, None, axis=dim), axis, forward
        )
        high = lax.ppermute(lax.slice_in_dim(block, 0, width, axis=dim), axis, backward)
        block = jnp.concatenate([low, block, high], axis=dim)
    return block


def mix(kernel, slab):
    return jnp.einsum("oi,ixyz->oxyz", kernel, slab, precision=lax.Precision.HIGHEST)


def contract(left, slab):
    return jnp.einsum("oxyz,ixyz->oi", left, slab, precision=lax.Precision.HIGHEST)


def shards(volume, weight, gamma, beta, cotangent):
    chans, cells_x, cells_y, cells_z = volume.shape
    count = float(
        cells_x
        * cells_y
        * cells_z
        * lax.axis_size("gx")
        * lax.axis_size("gy")
        * lax.axis_size("gz")
    )
    padded = with_halo(volume, (("gx", 1), ("gy", 2), ("gz", 3)), 1)

    def window(source, first, second, third):
        return source[
            :, first : first + cells_x, second : second + cells_y, third : third + cells_z
        ]

    conv = jnp.zeros(volume.shape, jnp.float32)
    for first in range(3):
        for second in range(3):
            for third in range(3):
                conv = conv + mix(
                    weight[:, :, first, second, third], window(padded, first, second, third)
                )
    first_sum, square_sum = lax.psum(
        (jnp.sum(conv, axis=(1, 2, 3)), jnp.sum(conv * conv, axis=(1, 2, 3))), ("gx", "gy", "gz")
    )
    mean = first_sum / count
    var = square_sum / count - mean * mean
    centred = conv - mean[:, None, None, None]
    rstd = lax.rsqrt(var + 1e-05)
    normed = centred * rstd[:, None, None, None]
    act = gamma[:, None, None, None] * normed + beta[:, None, None, None]
    sig = jax.nn.sigmoid(act)
    act_grad = cotangent * sig * (1.0 + act * (1.0 - sig))
    scale = gamma * rstd
    gamma_grad, beta_grad = lax.psum(
        (jnp.sum(act_grad * normed, axis=(1, 2, 3)), jnp.sum(act_grad, axis=(1, 2, 3))),
        ("gx", "gy", "gz"),
    )
    conv_grad = scale[:, None, None, None] * (
        act_grad
        - (beta_grad / count)[:, None, None, None]
        - normed * (gamma_grad / count)[:, None, None, None]
    )
    pieces = []
    for first in range(3):
        for second in range(3):
            for third in range(3):
                pieces.append(contract(conv_grad, window(padded, first, second, third)))
    weight_grad = lax.psum(
        jnp.stack(pieces, axis=2).reshape(chans, chans, 3, 3, 3), ("gx", "gy", "gz")
    )
    grad_padded = with_halo(conv_grad, (("gx", 1), ("gy", 2), ("gz", 3)), 1)
    input_grad = jnp.zeros(volume.shape, jnp.float32)
    for first in range(3):
        for second in range(3):
            for third in range(3):
                input_grad = input_grad + mix(
                    weight[:, :, first, second, third].T,
                    window(grad_padded, 2 - first, 2 - second, 2 - third),
                )
    return (input_grad, weight_grad, gamma_grad, beta_grad)


def solution(mesh):
    return jax.shard_map(
        shards,
        mesh=mesh,
        in_specs=(P(None, "gx", "gy", "gz"), P(), P(), P(), P(None, "gx", "gy", "gz")),
        out_specs=(P(None, "gx", "gy", "gz"), P(), P(), P()),
        check_vma=False,
    )
```

profile of v0, /device:TPU:1, one launch (start us, length us, event | category | flops | bytes accessed | tf_op | source)
XLA Modules:
  0.0 249.8 jit_solution(15097560473422288166)
XLA Ops:
  0.6 1.1 fusion.319
  1.7 2.1 collective-permute-start
  4.0 2.7 %fusion.206 = f32[16,4,16,128]{3,0,2,1:T(8,128)} fusion(f32[16,16,3,3,3]{1,0,4,3,2:T(8,128)} %param.6, f32[16,4,16,128]{3,2,1,0:T(8,128)} %param.5), kind=kOutput, calls=%fused_computation.290 | convolution fusion | flops 25165824 | bytes 1056768 | tf_op jit(solution)/shard_map/oi,ixyz->oxyz/dot_general | solution.py:22
  7.4 2.4 collective-permute-done.1
  9.9 1.3 collective-permute-start.2
  11.2 2.1 collective-permute-start.3
  13.3 2.1 fusion.225
  15.4 2.1 convolution_bitcast_fusion.4
  18.5 3.1 %collective-permute-start.4 = (f32[16,6,18,1]{2,0,3,1:T(8,128)S(1)}, f32[16,6,18,1]{2,0,3,1:T(8,128)S(1)}, u32[]{:S(2)}, u32[]{:S(2)}) collective-permute-start(f32[16,6,18,1]{2,0,3,1:T(8,128)S(1)} %copy.48), channel_id=1, source_target_pairs={{0,1},{1,2},{2,3},{3,0},{4,5},{5,6},{6,7},{7,4},{8,9},{9,10},{10,1... | collective-permute-start | bytes 20744 | tf_op jit(solution)/shard_map/ppermute | solution.py:13
  22.5 2.1 fusion.85
  24.6 2.1 fusion.86
  26.7 2.1 fusion.87
  28.7 2.1 convolution_bitcast_fusion.3
  30.8 2.1 convolution_bitcast_fusion.5
  32.8 2.1 convolution_bitcast_fusion.6
  35.6 1.6 copy.51
  37.2 1.8 maximum_maximum_fusion
  46.6 1.1 convolution_bitcast_fusion.18
  49.7 1.0 fusion.44
  51.2 1.2 fusion.312
  52.4 37.8 %all-reduce.1 = (f32[16]{0:T(128)S(1)}, f32[16]{0:T(128)S(1)}) all-reduce(f32[16]{0:T(128)S(1)} %get-tuple-element.15, f32[16]{0:T(128)S(1)} %get-tuple-element.14), channel_id=1, replica_groups=mesh['gx'=2,'gy'=4,'gz'=4] {'gx','gy','gz'}, use_global_device_ids=true, to_apply=%region_1.0 | all-reduce | flops 32 | bytes 256 | tf_op jit(solution)/shard_map/psum | solution.py:53
  90.2 2.4 fusion.311
  92.6 40.5 %all-reduce = (f32[16]{0:T(128)S(1)}, f32[16]{0:T(128)S(1)}) all-reduce(f32[16]{0:T(128)S(1)} %get-tuple-element.13, f32[16]{0:T(128)S(1)} %get-tuple-element.12), channel_id=1, replica_groups=mesh['gx'=2,'gy'=4,'gz'=4] {'gx','gy','gz'}, use_global_device_ids=true, to_apply=%region_7.0 | all-reduce | flops 32 | bytes 256 | tf_op jit(solution)/shard_map/psum | solution.py:65
  133.1 1.4 subtract_multiply_fusion
  136.8 0.9 fusion.75
  137.7 0.8 fusion.74
  139.3 0.9 fusion.72
  141.8 0.9 fusion.69
  142.7 0.8 fusion.68
  144.3 0.9 fusion.66
  145.2 0.8 fusion.65
  146.0 1.0 fusion.64
  147.0 0.9 fusion.63
  147.9 0.8 fusion.62
  149.5 0.9 fusion.60
  150.4 0.8 fusion.59
  152.0 0.9 fusion.57
  153.6 1.0 fusion.55
  154.6 0.9 fusion.54
  155.5 0.8 fusion.53
  157.1 0.9 fusion.51
  158.7 42.0 %psum.39 = f32[16,16,3,3,3]{1,0,4,3,2:T(8,128)} all-reduce(f32[16,16,3,3,3]{1,0,4,3,2:T(8,128)} %bitcast.644), channel_id=1, replica_groups=mesh['gx'=2,'gy'=4,'gz'=4] {'gx','gy','gz'}, use_global_device_ids=true, to_apply=%region_8.0 | all-reduce | flops 6912 | bytes 55296 | tf_op jit(solution)/shard_map/psum | solution.py:79
  200.9 1.3 collective-permute-start.7
  202.2 1.4 fusion.204
  203.6 0.9 collective-permute-done.6
  204.5 2.6 %collective-permute-done.7 = f32[16,1,16,128]{3,0,2,1:T(8,128)S(1)} collective-permute-done((f32[16,1,16,128]{3,0,2,1:T(8,128)S(1)}, f32[16,1,16,128]{3,0,2,1:T(8,128)S(1)}, u32[]{:S(2)}, u32[]{:S(2)}) %collective-permute-start.7) | collective-permute-done | bytes 131104 | tf_op jit(solution)/shard_map/ppermute | solution.py:16
  207.2 1.9 collective-permute-start.9
  209.1 1.4 fusion.78
  211.1 2.6 %collective-permute-done.8 = f32[16,6,1,128]{3,0,2,1:T(8,128)S(1)} collective-permute-done((f32[16,6,1,128]{3,0,2,1:T(8,128)S(1)}, f32[16,6,1,128]{3,0,2,1:T(8,128)S(1)}, u32[]{:S(2)}, u32[]{:S(2)}) %collective-permute-start.8) | collective-permute-done | bytes 49184 | tf_op jit(solution)/shard_map/ppermute | solution.py:13
  213.9 1.2 fusion.315
  215.1 1.8 copy.56
  216.9 3.8 %collective-permute-start.10 = (f32[16,6,18,1]{2,0,3,1:T(8,128)S(1)}, f32[16,6,18,1]{2,0,3,1:T(8,128)S(1)}, u32[]{:S(2)}, u32[]{:S(2)}) collective-permute-start(f32[16,6,18,1]{2,0,3,1:T(8,128)S(1)} %copy.56), channel_id=1, source_target_pairs={{1,0},{2,1},{3,2},{0,3},{5,4},{6,5},{7,6},{4,7},{9,8},{10,9},{11,1... | collective-permute-start | bytes 20744 | tf_op jit(solution)/shard_map/ppermute | solution.py:16
  221.7 1.4 fusion.177
  223.1 1.4 fusion.175
  224.5 1.4 fusion.176
  225.9 1.4 fusion.174
  227.3 1.4 convolution_bitcast_fusion.2
  228.7 1.4 convolution_bitcast_fusion
  230.1 1.6 copy.57
  231.7 1.6 copy.61
  233.3 2.0 pad_maximum_fusion.3
  246.2 1.1 fusion.46
  247.6 1.0 fusion.48
  248.6 1.0 copy.88
  (142 shorter events, 35.4 us)
Async XLA Ops:
  0.6 6.4 %copy-start.2 = (f32[16,4,16,128]{3,2,1,0:T(8,128)S(1)}, f32[16,4,16,128]{3,2,1,0:T(8,128)}, u32[]{:S(2)}) copy-start(f32[16,4,16,128]{3,2,1,0:T(8,128)} %param.5) | copy-start | bytes 1572868
  1.7 5.3 %collective-permute-start = (f32[16,1,16,128]{3,0,2,1:T(8,128)S(1)}, f32[16,1,16,128]{3,0,2,1:T(8,128)S(1)}, u32[]{:S(2)}, u32[]{:S(2)}) collective-permute-start(f32[16,1,16,128]{3,0,2,1:T(8,128)S(1)} %copy.207), channel_id=1, source_target_pairs={{0,16},{16,0},{1,17},{17,1},{2,18},{18,2},{3,19},{19,3},{4,20},{20... | collective-permute-start | bytes 393224 | tf_op jit(solution)/shard_map/ppermute | solution.py:13
  3.9 6.0 %collective-permute-start.1 = (f32[16,1,16,128]{3,0,2,1:T(8,128)S(1)}, f32[16,1,16,128]{3,0,2,1:T(8,128)S(1)}, u32[]{:S(2)}, u32[]{:S(2)}) collective-permute-start(f32[16,1,16,128]{3,0,2,1:T(8,128)S(1)} %copy.208), channel_id=1, source_target_pairs={{16,0},{0,16},{17,1},{1,17},{18,2},{2,18},{19,3},{3,19},{20,4},{4,... | collective-permute-start | bytes 393224 | tf_op jit(solution)/shard_map/ppermute | solution.py:16
  7.4 10.0 %copy-start.7 = (f32[16,5,16,128]{3,0,2,1:T(8,128)}, f32[16,5,16,128]{3,0,2,1:T(8,128)S(1)}, u32[]{:S(2)}) copy-start(f32[16,5,16,128]{3,0,2,1:T(8,128)S(1)} %get-tuple-element.37) | copy-start | bytes 1966084
  9.9 7.6 %copy-start.5 = (f32[16,5,16,128]{3,0,2,1:T(8,128)}, f32[16,5,16,128]{3,0,2,1:T(8,128)S(1)}, u32[]{:S(2)}) copy-start(f32[16,5,16,128]{3,0,2,1:T(8,128)S(1)} %get-tuple-element.44) | copy-start | bytes 1966084
  9.9 7.5 %collective-permute-start.2 = (f32[16,6,1,128]{3,0,2,1:T(8,128)S(1)}, f32[16,6,1,128]{3,0,2,1:T(8,128)S(1)}, u32[]{:S(2)}, u32[]{:S(2)}) collective-permute-start(f32[16,6,1,128]{3,0,2,1:T(8,128)S(1)} %get-tuple-element.33), channel_id=1, source_target_pairs={{0,4},{4,8},{8,12},{12,0},{1,5},{5,9},{9,13},{13,1},{2,6},{6,10},{... | collective-permute-start | bytes 147464 | tf_op jit(solution)/shard_map/ppermute | solution.py:13
  11.2 6.2 %collective-permute-start.3 = (f32[16,6,1,128]{3,0,2,1:T(8,128)S(1)}, f32[16,6,1,128]{3,0,2,1:T(8,128)S(1)}, u32[]{:S(2)}, u32[]{:S(2)}) collective-permute-start(f32[16,6,1,128]{3,0,2,1:T(8,128)S(1)} %get-tuple-element.34), channel_id=1, source_target_pairs={{4,0},{8,4},{12,8},{0,12},{5,1},{9,5},{13,9},{1,13},{6,2},{10,6},{... | collective-permute-start | bytes 147464 | tf_op jit(solution)/shard_map/ppermute | solution.py:16
  18.5 16.4 %collective-permute-start.4 = (f32[16,6,18,1]{2,0,3,1:T(8,128)S(1)}, f32[16,6,18,1]{2,0,3,1:T(8,128)S(1)}, u32[]{:S(2)}, u32[]{:S(2)}) collective-permute-start(f32[16,6,18,1]{2,0,3,1:T(8,128)S(1)} %copy.48), channel_id=1, source_target_pairs={{0,1},{1,2},{2,3},{3,0},{4,5},{5,6},{6,7},{7,4},{8,9},{9,10},{10,1... | collective-permute-start | bytes 20744 | tf_op jit(solution)/shard_map/ppermute | solution.py:13
  22.3 13.3 %collective-permute-start.5 = (f32[16,6,18,1]{2,0,3,1:T(8,128)S(1)}, f32[16,6,18,1]{2,0,3,1:T(8,128)S(1)}, u32[]{:S(2)}, u32[]{:S(2)}) collective-permute-start(f32[16,6,18,1]{2,0,3,1:T(8,128)S(1)} %copy.50), channel_id=1, source_target_pairs={{1,0},{2,1},{3,2},{0,3},{5,4},{6,5},{7,6},{4,7},{9,8},{10,9},{11,1... | collective-permute-start | bytes 20744 | tf_op jit(solution)/shard_map/ppermute | solution.py:16
  37.2 1.8 copy-start.26
  39.1 11.6 %copy-start = (f32[16,6,18,129]{3,0,2,1:T(8,128)}, f32[16,6,18,129]{3,0,2,1:T(8,128)S(1)}, u32[]{:S(2)}) copy-start(f32[16,6,18,129]{3,0,2,1:T(8,128)S(1)} %get-tuple-element.28) | copy-start | bytes 2674948
  47.7 1.9 copy-start.11
  47.7 1.9 copy-start.12
  47.8 1.9 copy-start.23
  47.8 1.9 copy-start.24
  47.8 1.9 copy-start.25
  49.7 1.0 copy-start.9
  49.7 1.2 copy-start.17
  49.7 1.3 copy-start.18
  49.7 1.5 copy-start.19
  51.2 39.0 %copy-start.31 = (f32[16]{0:T(128)S(1)}, f32[16]{0:T(128)}, u32[]{:S(2)}) copy-start(f32[16]{0:T(128)} %param.7) | copy-start | bytes 196
  51.2 39.0 %copy-start.32 = (f32[16]{0:T(128)S(1)}, f32[16]{0:T(128)}, u32[]{:S(2)}) copy-start(f32[16]{0:T(128)} %param.8) | copy-start | bytes 196
  52.4 80.8 %copy-start.4 = (f32[16,4,16,128]{3,0,2,1:T(8,128)}, f32[16,4,16,128]{3,0,2,1:T(8,128)S(1)}, u32[]{:S(2)}) copy-start(f32[16,4,16,128]{3,0,2,1:T(8,128)S(1)} %get-tuple-element.47) | copy-start | bytes 1572868
  133.1 3.7 %copy-start.33 = (f32[16]{0:T(128)}, f32[16]{0:T(128)S(1)}, u32[]{:S(2)}) copy-start(f32[16]{0:T(128)S(1)} %get-tuple-element.16) | copy-start | bytes 196
  133.1 3.7 %copy-start.34 = (f32[16]{0:T(128)}, f32[16]{0:T(128)S(1)}, u32[]{:S(2)}) copy-start(f32[16]{0:T(128)S(1)} %get-tuple-element.17) | copy-start | bytes 196
  134.5 2.3 copy-start.1
  136.0 2.5 copy-start.8
  143.5 2.5 %copy-start.3 = (f32[16,4,16,128]{3,2,1,0:T(8,128)S(1)}, f32[16,4,16,128]{3,2,1,0:T(8,128)}, u32[]{:S(2)}) copy-start(f32[16,4,16,128]{3,2,1,0:T(8,128)} %param.5) | copy-start | bytes 1572868
  151.2 2.5 copy-start.6
  155.5 46.7 %copy-start.27 = (f32[16,16,3,3,3]{1,0,4,3,2:T(8,128)S(1)}, f32[16,16,3,3,3]{1,0,4,3,2:T(8,128)}, u32[]{:S(2)}) copy-start(f32[16,16,3,3,3]{1,0,4,3,2:T(8,128)} %param.6) | copy-start | bytes 82948
  156.3 44.4 %copy-start.30 = (f32[16,1,16,128]{3,0,2,1:T(8,128)S(1)}, f32[16,1,16,128]{3,0,2,1:T(8,128)}, u32[]{:S(2)}) copy-start(f32[16,1,16,128]{3,0,2,1:T(8,128)} %get-tuple-element.35) | copy-start | bytes 393220
  156.3 44.6 %copy-start.29 = (f32[16,1,16,128]{3,0,2,1:T(8,128)S(1)}, f32[16,1,16,128]{3,0,2,1:T(8,128)}, u32[]{:S(2)}) copy-start(f32[16,1,16,128]{3,0,2,1:T(8,128)} %get-tuple-element.36) | copy-start | bytes 393220
  158.0 0.7 copy-start.28
  200.7 3.8 %collective-permute-start.6 = (f32[16,1,16,128]{3,0,2,1:T(8,128)S(1)}, f32[16,1,16,128]{3,0,2,1:T(8,128)S(1)}, u32[]{:S(2)}, u32[]{:S(2)}) collective-permute-start(f32[16,1,16,128]{3,0,2,1:T(8,128)S(1)} %copy-done.30), channel_id=1, source_target_pairs={{0,16},{16,0},{1,17},{17,1},{2,18},{18,2},{3,19},{19,3},{4,20},{20... | collective-permute-start | bytes 393224 | tf_op jit(solution)/shard_map/ppermute | solution.py:13
  200.9 6.3 %collective-permute-start.7 = (f32[16,1,16,128]{3,0,2,1:T(8,128)S(1)}, f32[16,1,16,128]{3,0,2,1:T(8,128)S(1)}, u32[]{:S(2)}, u32[]{:S(2)}) collective-permute-start(f32[16,1,16,128]{3,0,2,1:T(8,128)S(1)} %copy-done.29), channel_id=1, source_target_pairs={{16,0},{0,16},{17,1},{1,17},{18,2},{2,18},{19,3},{3,19},{20,4},{4,... | collective-permute-start | bytes 393224 | tf_op jit(solution)/shard_map/ppermute | solution.py:16
  207.2 4.0 %collective-permute-start.9 = (f32[16,6,1,128]{3,0,2,1:T(8,128)S(1)}, f32[16,6,1,128]{3,0,2,1:T(8,128)S(1)}, u32[]{:S(2)}, u32[]{:S(2)}) collective-permute-start(f32[16,6,1,128]{3,0,2,1:T(8,128)S(1)} %get-tuple-element.32), channel_id=1, source_target_pairs={{4,0},{8,4},{12,8},{0,12},{5,1},{9,5},{13,9},{1,13},{6,2},{10,6},{... | collective-permute-start | bytes 147464 | tf_op jit(solution)/shard_map/ppermute | solution.py:16
  209.1 4.7 %collective-permute-start.8 = (f32[16,6,1,128]{3,0,2,1:T(8,128)S(1)}, f32[16,6,1,128]{3,0,2,1:T(8,128)S(1)}, u32[]{:S(2)}, u32[]{:S(2)}) collective-permute-start(f32[16,6,1,128]{3,0,2,1:T(8,128)S(1)} %get-tuple-element.31), channel_id=1, source_target_pairs={{0,4},{4,8},{8,12},{12,0},{1,5},{5,9},{9,13},{13,1},{2,6},{6,10},{... | collective-permute-start | bytes 147464 | tf_op jit(solution)/shard_map/ppermute | solution.py:13
  216.9 13.2 %collective-permute-start.10 = (f32[16,6,18,1]{2,0,3,1:T(8,128)S(1)}, f32[16,6,18,1]{2,0,3,1:T(8,128)S(1)}, u32[]{:S(2)}, u32[]{:S(2)}) collective-permute-start(f32[16,6,18,1]{2,0,3,1:T(8,128)S(1)} %copy.56), channel_id=1, source_target_pairs={{1,0},{2,1},{3,2},{0,3},{5,4},{6,5},{7,6},{4,7},{9,8},{10,9},{11,1... | collective-permute-start | bytes 20744 | tf_op jit(solution)/shard_map/ppermute | solution.py:16
  221.4 10.3 %collective-permute-start.11 = (f32[16,6,18,1]{2,0,3,1:T(8,128)S(1)}, f32[16,6,18,1]{2,0,3,1:T(8,128)S(1)}, u32[]{:S(2)}, u32[]{:S(2)}) collective-permute-start(f32[16,6,18,1]{2,0,3,1:T(8,128)S(1)} %copy.60), channel_id=1, source_target_pairs={{0,1},{1,2},{2,3},{3,0},{4,5},{5,6},{6,7},{7,4},{8,9},{9,10},{10,1... | collective-permute-start | bytes 20744 | tf_op jit(solution)/shard_map/ppermute | solution.py:13
  243.9 2.3 copy-start.10
  243.9 2.3 copy-start.13
  243.9 2.3 copy-start.20
  244.1 2.1 copy-start.21
  244.1 2.1 copy-start.22
  246.2 1.1 copy-start.14
  246.2 1.2 copy-start.15
  246.2 1.3 copy-start.16
where the time goes:
time: 255 us; the launch traced here: 250 us
  blocking collectives  120 us (47%)
  matrix products  78.7 us (31%)
  starting transfers between devices  16.4 us (6%)
  local copies, waits for them, and re-layouts  15.7 us (6%)
  waiting for transfers between devices  9.06 us (4%)
  other arithmetic  7.77 us (3%)
    dot_general x54, matrix products, mix(): jnp.einsum('oi,ixyz->oxyz', kernel, slab, precision=lax.Precision.HIGHEST)  56 us
    psum x1, blocking collectives, shards(): lax.psum(jnp.stack(pieces, axis=2).reshape(chans, chans, 3, 3, 3), ('gx',...  42 us
    psum x1, blocking collectives, shards(): lax.psum((jnp.sum(act_grad * normed, axis=(1, 2, 3)), jnp.sum(act_grad, a...  40.5 us
    psum x1, blocking collectives, shards(): lax.psum((jnp.sum(conv, axis=(1, 2, 3)), jnp.sum(conv * conv, axis=(1, 2,...  37.8 us
    dot_general x27, matrix products, contract(): jnp.einsum('oxyz,ixyz->oi', left, slab, precision=lax.Precision.HIGHEST)  22.7 us
    ppermute x6, starting transfers between devices, with_halo(): lax.ppermute(lax.slice_in_dim(block, 0, width, axis=dim), axis, backward)  9.35 us
    ppermute x6, starting transfers between devices, with_halo(): lax.ppermute(lax.slice_in_dim(block, block.shape[dim] - width, None, axis...  7.05 us
  transfers between devices with their start and end apart: 12, of which 5 were waited for; matrix products, arithmetic and copies ran while one was open for 14% of the time, Pallas kernels for 0%

commit v1 on v0

v1 whole, which is shorter than its diff:
```python
import functools

import jax
import jax.numpy as jnp
from jax import lax
from jax.experimental import pallas as pl
from jax.experimental.pallas import tpu as pltpu
from jax.sharding import PartitionSpec as P

AXES = ("gx", "gy", "gz")
F32, BF16 = jnp.float32, jnp.bfloat16


def call(body, outs, scratch=(), name=None):
    return pl.pallas_call(
        body,
        out_shape=[jax.ShapeDtypeStruct(shape, kind) for shape, kind in outs],
        scratch_shapes=list(scratch),
        name=name,
        compiler_params=pltpu.CompilerParams(vmem_limit_bytes=60 * 2**20),
    )


def turns(count):
    forward = [(i, (i + 1) % count) for i in range(count)]
    return forward, [(target, source) for source, target in forward]


def joint(first, second, wide):
    return [(a * wide + b, c * wide + d) for a, c in first for b, d in second]


def faces(store, field, x, y, size_x, size_y, value):
    grid, x_face, y_low, y_high, xy_low, xy_high = store
    grid[field, x, y] = value
    sides = ([0] if x == 0 else []) + ([1] if x == size_x - 1 else [])
    for side in sides:
        x_face[side, field, y] = value
    for edge, line, corner in ((0, y_low, xy_low), (size_y - 1, y_high, xy_high)):
        if y == edge:
            line[field, x] = value
            for side in sides:
                corner[side, field] = value


def face_shapes(fields, dims):
    size_x, size_y, chans, size_z = dims
    return [
        ((fields, size_x, size_y, chans, size_z), F32),
        ((2, fields, size_y, chans, size_z), F32),
        ((fields, size_x, chans, size_z), F32),
        ((fields, size_x, chans, size_z), F32),
        ((2, fields, chans, size_z), F32),
        ((2, fields, chans, size_z), F32),
    ]


def split_faces(dims, volume, *store):
    size_x, size_y, chans, size_z = dims
    for x in range(size_x):
        for y in range(size_y):
            value = volume[pl.ds(x * size_y + y, chans, stride=size_x * size_y), :]
            faces(store, 0, x, y, size_x, size_y, value)


def pad_kernel(fields, dims, grid, x_face, y_low, y_high, xy_low, xy_high, padded, first, last):
    size_x, size_y, chans, size_z = dims
    wide = size_y + 2
    pairs = padded.shape[1]
    group = 128 // chans
    for field in range(fields):
        for x in range(size_x):
            padded[field, pl.ds((x + 1) * wide + 1, size_y)] = grid[field, x]
            padded[field, (x + 1) * wide] = y_low[field, x]
            padded[field, (x + 1) * wide + size_y + 1] = y_high[field, x]
        for side, row in ((1, 0), (0, size_x + 1)):
            padded[field, pl.ds(row * wide + 1, size_y)] = x_face[side, field]
            padded[field, row * wide] = xy_low[side, field]
            padded[field, row * wide + size_y + 1] = xy_high[side, field]
        used = (size_x + 2) * wide
        if pairs > used:
            padded[field, pl.ds(used, pairs - used)] = jnp.zeros((pairs - used, chans, size_z), F32)
        rows = first.shape[0] // fields
        for at in range(pairs // group):
            block = padded[field, pl.ds(at * group, group)].reshape(group * chans, size_z)
            turned = block.T
            first[field * rows + at : field * rows + at + 1] = turned[:1]
            last[field * rows + at : field * rows + at + 1] = turned[size_z - 1 :]


def exchange(fields, dims, grid, x_face, y_low, y_high, xy_low, xy_high):
    size_x, size_y, chans, size_z = dims
    count_x, count_y, count_z = (lax.axis_size(axis) for axis in AXES)
    up_x, down_x = turns(count_x)
    up_y, down_y = turns(count_y)
    up_z, down_z = turns(count_z)

    def over_x(pieces, second, axes):
        def pairs(first):
            return first if second is None else joint(first, second, count_y)

        if count_x == 2:
            return lax.ppermute(pieces, axes, pairs(up_x))
        return jnp.stack(
            [lax.ppermute(pieces[0], axes, pairs(down_x)), lax.ppermute(pieces[1], axes, pairs(up_x))]
        )

    x_halo = over_x(x_face, None, "gx")
    low = lax.ppermute(y_high, "gy", up_y)
    high = lax.ppermute(y_low, "gy", down_y)
    xy_low_halo = over_x(xy_high, up_y, ("gx", "gy"))
    xy_high_halo = over_x(xy_low, down_y, ("gx", "gy"))
    group = 128 // chans
    groups = -(-(size_x + 2) * (size_y + 2) // group)
    rows = -(-groups // 8) * 8
    padded, first, last = call(
        functools.partial(pad_kernel, fields, dims),
        [
            ((fields, groups * group, chans, size_z), F32),
            ((fields * rows, 128), F32),
            ((fields * rows, 128), F32),
        ],
        name="pad_faces",
    )(grid, x_halo, low, high, xy_low_halo, xy_high_halo)
    before = lax.ppermute(last, "gz", up_z)
    after = lax.ppermute(first, "gz", down_z)
    return padded, before, after


def halo_block(before, after, row, size_z):
    rows = jnp.concatenate(
        [
            after[pl.ds(row, 1), :],
            jnp.zeros((size_z - 2, 128), F32),
            before[pl.ds(row, 1), :],
        ],
        axis=0,
    )
    return rows.T


def put_shifts(pair, value, edge, high, low):
    chans, size_z = value.shape
    lane = lax.broadcasted_iota(jnp.int32, value.shape, 1)
    left = pltpu.roll(jnp.where(lane == size_z - 1, edge, value), 1, 1)
    right = pltpu.roll(jnp.where(lane == 0, edge, value), size_z - 1, 1)
    for tap, part in enumerate((left, value, right)):
        top = part.astype(BF16)
        high[pair, tap * chans : (tap + 1) * chans] = top
        low[pair, tap * chans : (tap + 1) * chans] = (part - top.astype(F32)).astype(BF16)


def window(source, x, y, wide, count):
    columns = []
    for at in range(count):
        rows = []
        for first in range(3):
            block = source[pl.ds((x + first) * wide + y + at, 3)]
            rows.append(block.reshape(3 * block.shape[1], block.shape[2]))
        columns.append(jnp.concatenate(rows, axis=0))
    return jnp.concatenate(columns, axis=1)


def product(both, top, high, low, x, y, wide, count):
    chans = top.shape[0]
    wide_part = jnp.dot(both, window(high, x, y, wide, count), preferred_element_type=F32)
    thin_part = jnp.dot(top, window(low, x, y, wide, count), preferred_element_type=F32)
    return wide_part[:chans] + (wide_part[chans:] + thin_part)


def conv_kernel(dims, padded, before, after, both, top, conv, high, low, stats):
    size_x, size_y, chans, size_z = dims
    wide = size_y + 2
    group = 128 // chans

    def shifts(at, _):
        edges = halo_block(before, after, at, size_z)
        for one in range(group):
            pair = at * group + one
            edge = edges[one * chans : (one + 1) * chans]
            put_shifts(pair, padded[0, pair], edge, high, low)
        return 0

    lax.fori_loop(0, padded.shape[1] // group, shifts, 0)
    width = 2
    both_now, top_now = both[...], top[...]

    def step(at, carry):
        x, y = at // (size_y // width), (at % (size_y // width)) * width
        out = product(both_now, top_now, high, low, x, y, wide, width)
        total, source = carry
        for one in range(width):
            part = out[:, one * size_z : (one + 1) * size_z]
            conv[x, y + one] = part
            total = total + part
            source = source + padded[0, (x + 1) * wide + 1 + y + one]
        return total, source

    zero = jnp.zeros((chans, size_z), F32)
    total, source = lax.fori_loop(0, size_x * size_y // width, step, (zero, zero))
    sums = jnp.sum(total, axis=1, keepdims=True)
    centre = sums * (1.0 / (size_x * size_y * size_z))

    def spread(x, squares):
        for y in range(size_y):
            away = conv[x, y] - centre
            squares = squares + away * away
        return squares

    squares = lax.fori_loop(0, size_x, spread, zero)
    lane = lax.broadcasted_iota(jnp.int32, (chans, 128), 1)
    table = jnp.where(
        lane == 0,
        sums,
        jnp.where(
            lane == 1,
            jnp.sum(squares, axis=1, keepdims=True),
            jnp.where(lane == 2, jnp.sum(source, axis=1, keepdims=True), 0.0),
        ),
    )
    full = jnp.concatenate([table, jnp.zeros((128 - chans, 128), F32)], axis=0).T
    row = full[0:1] + pltpu.roll(full[1:2], chans, 1) + pltpu.roll(full[2:3], 2 * chans, 1)
    stats[...] = jnp.broadcast_to(row, stats.shape)


def act_kernel(dims, count, conv, cotangent, high, low, stats, gamma, beta, *outs):
    size_x, size_y, chans, size_z = dims
    store, sums, scales = outs[:6], outs[6], outs[7]
    local = float(size_x * size_y * size_z)
    wide = size_y + 2
    rows = stats[...]
    lane = lax.broadcasted_iota(jnp.int32, rows.shape, 1)
    mean_row = jnp.sum(rows, axis=0, keepdims=True) * (1.0 / count)
    away = jnp.where(lane < chans, rows * (1.0 / local) - mean_row, 0.0)
    spread_row = jnp.sum(away * away, axis=0, keepdims=True) * (local / count)
    var_row = mean_row + pltpu.roll(spread_row, chans, 1)
    rstd_row = lax.rsqrt(var_row + 1e-05)
    table = jnp.concatenate([mean_row, rstd_row, jnp.zeros((126, 128), F32)], axis=0).T
    mean = table[:chans, 0:1]
    rstd = table[chans : 2 * chans, 1:2]
    level = table[2 * chans : 3 * chans, 0:1]
    gain, shift = gamma[...], beta[...]
    scales[...] = jnp.broadcast_to(gain * rstd, scales.shape)
    gamma_sum = jnp.zeros((chans, size_z), F32)
    beta_sum = jnp.zeros((chans, size_z), F32)
    for x in range(size_x):
        for y in range(size_y):
            normed = (conv[x, y] - mean) * rstd
            act = gain * normed + shift
            sig = 1.0 / (1.0 + jnp.exp(-act))
            pull = cotangent[pl.ds(x * size_y + y, chans, stride=size_x * size_y), :]
            grad = pull * sig * (1.0 + act * (1.0 - sig))
            gamma_sum = gamma_sum + grad * normed
            beta_sum = beta_sum + grad
            faces(store, 0, x, y, size_x, size_y, grad)
            faces(store, 1, x, y, size_x, size_y, normed)
    gamma_part = jnp.sum(gamma_sum, axis=1, keepdims=True)
    beta_part = jnp.sum(beta_sum, axis=1, keepdims=True)
    centre = beta_part * (1.0 / local)
    grid = store[0]
    width = 4
    ones = jnp.ones((chans, size_z), BF16)

    def step(at, total):
        x, y = at // (size_y // width), (at % (size_y // width)) * width
        columns = []
        for one in range(width):
            grad = grid[0, x, y + one] - centre
            normed = grid[1, x, y + one]
            grad_top = grad.astype(BF16)
            normed_top = normed.astype(BF16)
            columns.append(
                jnp.concatenate(
                    [
                        grad_top,
                        (grad - grad_top.astype(F32)).astype(BF16),
                        normed_top,
                        (normed - normed_top.astype(F32)).astype(BF16),
                        ones,
                    ],
                    axis=0,
                )
            )
        right = jnp.concatenate(columns, axis=1)
        dims_in = (((1,), (1,)), ((), ()))
        for part in (high, low):
            left = window(part, x, y, wide, width)
            total = total + lax.dot_general(left, right, dims_in, preferred_element_type=F32)
        return total

    taps = 27 * chans
    total = lax.fori_loop(
        0, size_x * size_y // width, step, jnp.zeros((taps, 5 * chans), F32)
    )
    tall = -(-taps // 128) * 128
    levels = jnp.concatenate([level] * 27, axis=0)
    spare = 128 - 5 * chans
    side = jnp.concatenate([total, jnp.broadcast_to(levels, (taps, spare))], axis=1)
    side = jnp.concatenate([side, jnp.zeros((tall - taps, 128), F32)], axis=0)
    turned = jnp.concatenate(
        [side[at : at + 128].T for at in range(0, tall, 128)], axis=1
    )
    drift = turned[4 * chans : 4 * chans + 1] - local * turned[5 * chans : 5 * chans + 1]
    main = turned[:chans] + turned[chans : 2 * chans] + centre * drift
    other = turned[2 * chans : 3 * chans] + turned[3 * chans : 4 * chans]
    lane = lax.broadcasted_iota(jnp.int32, main.shape, 1)
    main = jnp.where(lane == taps, gamma_part, jnp.where(lane == taps + 1, beta_part, main))
    sums[0:chans] = main
    sums[chans : 2 * chans] = other


def grad_kernel(dims, count, padded, before, after, sums, scales, both, top, out, weight_grad, high, low):
    size_x, size_y, chans, size_z = dims
    wide = size_y + 2
    group = 128 // chans
    taps = 27 * chans
    scale = scales[...]
    main, other = sums[0:chans], sums[chans : 2 * chans]
    gamma_mean = main[:, taps : taps + 1] * (1.0 / count)
    beta_mean = main[:, taps + 1 : taps + 2] * (1.0 / count)
    weight_grad[...] = scale[:, 0:1] * (main - gamma_mean * other)
    gamma_wide = jnp.broadcast_to(gamma_mean, (chans, size_z))
    beta_wide = jnp.broadcast_to(beta_mean, (chans, size_z))
    rows = before.shape[0] // 2

    def mixed(grad, normed):
        return scale * (grad - beta_wide - normed * gamma_wide)

    def shifts(at, _):
        edge_grad = halo_block(before, after, at, size_z)
        edge_normed = halo_block(before, after, rows + at, size_z)
        for one in range(group):
            pair = at * group + one
            part = slice(one * chans, (one + 1) * chans)
            value = mixed(padded[0, pair], padded[1, pair])
            edge = mixed(edge_grad[part], edge_normed[part])
            put_shifts(pair, value, edge, high, low)
        return 0

    lax.fori_loop(0, padded.shape[1] // group, shifts, 0)
    width = 2
    both_now, top_now = both[...], top[...]
    stride = size_x * size_y

    def step(at, _):
        x, y = at // (size_y // width), (at % (size_y // width)) * width
        value = product(both_now, top_now, high, low, x, y, wide, width)
        for one in range(width):
            out[pl.ds(x * size_y + y + one, chans, stride=stride), :] = value[
                :, one * size_z : (one + 1) * size_z
            ]
        return 0

    lax.fori_loop(0, size_x * size_y // width, step, 0)


def total_over(value):
    for axis in ("gz", "gx", "gy"):
        count = lax.axis_size(axis)
        if count & (count - 1):
            value = lax.psum(value, axis)
            continue
        step = 1
        while step < count:
            value = value + lax.ppermute(value, axis, [(i, i ^ step) for i in range(count)])
            step *= 2
    return value


def two_parts(table):
    top = lax.reduce_precision(table, 8, 7)
    rest = (table - top).astype(BF16)
    top = top.astype(BF16)
    return jnp.concatenate([top, rest], axis=0), top


def shards(volume, weight, gamma, beta, cotangent):
    chans, size_x, size_y, size_z = volume.shape
    devices = 1
    for axis in AXES:
        devices *= lax.axis_size(axis)
    dims = (size_x, size_y, chans, size_z)
    count = float(size_x * size_y * size_z * devices)
    taps = 27 * chans
    tall = -(-taps // 128) * 128
    flat = (chans * size_x * size_y, size_z)
    store = call(functools.partial(split_faces, dims), face_shapes(1, dims), name="faces")(
        volume.reshape(flat)
    )
    padded, before, after = exchange(1, dims, *store)
    both, top = two_parts(weight.transpose(0, 2, 3, 4, 1).reshape(chans, taps))
    back = weight[:, :, ::-1, ::-1, ::-1].transpose(1, 2, 3, 4, 0).reshape(chans, taps)
    back_both, back_top = two_parts(back)
    pairs = padded.shape[1]
    conv, high, low, stats = call(
        functools.partial(conv_kernel, dims),
        [
            ((size_x, size_y, chans, size_z), F32),
            ((pairs, 3 * chans, size_z), BF16),
            ((pairs, 3 * chans, size_z), BF16),
            ((devices, 128), F32),
        ],
        name="conv",
    )(padded, before, after, both, top)
    stats = lax.all_to_all(stats, AXES, 0, 0, tiled=True)
    *store, sums, scales = call(
        functools.partial(act_kernel, dims, count),
        face_shapes(2, dims) + [((2 * chans, tall), F32), ((chans, size_z), F32)],
        name="act",
    )(conv, cotangent.reshape(flat), high, low, stats, gamma[:, None], beta[:, None])
    padded, before, after = exchange(2, dims, *store)
    sums = total_over(sums)
    input_grad, weight_grad = call(
        functools.partial(grad_kernel, dims, count),
        [(flat, F32), ((chans, tall), F32)],
        scratch=[
            pltpu.VMEM((pairs, 3 * chans, size_z), BF16),
            pltpu.VMEM((pairs, 3 * chans, size_z), BF16),
        ],
        name="grads",
    )(padded, before, after, sums, scales, back_both, back_top)
    weight_grad = weight_grad[:, :taps].reshape(chans, 3, 3, 3, chans).transpose(0, 4, 1, 2, 3)
    return (
        input_grad.reshape(volume.shape),
        weight_grad,
        sums[:chans, taps],
        sums[:chans, taps + 1],
    )


def solution(mesh):
    return jax.shard_map(
        shards,
        mesh=mesh,
        in_specs=(P(None, "gx", "gy", "gz"), P(), P(), P(), P(None, "gx", "gy", "gz")),
        out_specs=(P(None, "gx", "gy", "gz"), P(), P(), P()),
        check_vma=False,
    )
```

time: 255 us -> 116 us (0.45); the launches traced: 250 us -> 115 us
  blocking collectives: 120 us -> 0 us
  matrix products: 78.7 us -> 0 us
  Pallas kernels: 0 us -> 40.2 us
  waiting for transfers between devices: 9.06 us -> 31.6 us
  starting transfers between devices: 16.4 us -> 32 us
  local copies, waits for them, and re-layouts: 15.7 us -> 8.37 us
  other arithmetic: 7.77 us -> 2.14 us
    psum x3 -> x0, blocking collectives: 120 us -> none  [the longest x1 42 us: shards(): lax.psum(jnp.stack(pieces, axis=2).reshape(chans, chans, 3, 3, 3), ('gx',...]
    dot_general x81 -> x0, matrix products: 78.7 us -> none  [the longest x54 56 us: mix(): jnp.einsum('oi,ixyz->oxyz', kernel, slab, precision=lax.Precision.HIGHEST)]
    pallas_call x0 -> x6, Pallas kernels: none -> 40.2 us  [the longest x1 11.6 us: shards(): call(functools.partial(conv_kernel, dims), [((size_x, size_y, chans, size...]
    ppermute x12 -> x19, waiting for transfers between devices: 9.06 us -> 26.1 us  [the longest x5 19.4 us: total_over(): lax.ppermute(value, axis, [(i, i ^ step) for i in range(count)])]
    ppermute x12 -> x19, starting transfers between devices: 16.4 us -> 27.1 us  [the longest x2 9.5 us: exchange(): before = lax.ppermute(last, 'gz', up_z)]
    slice x9 -> x1, local copies, waits for them, and re-layouts: 7.16 us -> 0.7 us  [shards(): sums[:chans, taps + 1]]
    ppermute x4 -> x0, local copies, waits for them, and re-layouts: 5.49 us -> none  [the longest x2 3.2 us: with_halo(): lax.ppermute(lax.slice_in_dim(block, 0, width, axis=dim), axis, backward)]
    all_to_all x0 -> x1, waiting for transfers between devices: none -> 5.44 us  [shards(): stats = lax.all_to_all(stats, AXES, 0, 0, tiled=True)]
  transfers between devices with their start and end apart: 12 -> 20, of which waited for: 5 -> 13; matrix products, arithmetic and copies ran while one was open for 14% -> 4% of each run, Pallas kernels for 0% -> 0%
where the time goes in v1:
time: 116 us; the launch traced here: 115 us
  Pallas kernels  40.2 us (35%)
  starting transfers between devices  32 us (28%)
  waiting for transfers between devices  31.6 us (27%)
  local copies, waits for them, and re-layouts  8.37 us (7%)
  other arithmetic  2.14 us (2%)
    ppermute x5, waiting for transfers between devices, total_over(): lax.ppermute(value, axis, [(i, i ^ step) for i in range(count)])  19.4 us
    pallas_call x1, Pallas kernels, shards(): call(functools.partial(conv_kernel, dims), [((size_x, size_y, chans, size...  11.6 us
    pallas_call x1, Pallas kernels, shards(): call(functools.partial(grad_kernel, dims, count), [(flat, F32), ((chans,...  11.1 us
    pallas_call x1, Pallas kernels, shards(): call(functools.partial(act_kernel, dims, count), face_shapes(2, dims) + [...  9.95 us
    ppermute x2, starting transfers between devices, exchange(): before = lax.ppermute(last, 'gz', up_z)  9.5 us
    ppermute x6, starting transfers between devices, over_x(): return lax.ppermute(pieces, axes, pairs(up_x))  8.78 us
    all_to_all x1, waiting for transfers between devices, shards(): stats = lax.all_to_all(stats, AXES, 0, 0, tiled=True)  5.44 us
    pallas_call x2, Pallas kernels, exchange(): call(functools.partial(pad_kernel, fields, dims), [((fields, groups * gro...  5.34 us
  transfers between devices with their start and end apart: 20, of which 13 were waited for; matrix products, arithmetic and copies ran while one was open for 4% of the time, Pallas kernels for 0%

profile of v1, /device:TPU:1, one launch (start us, length us, event | category | flops | bytes accessed | tf_op | source)
XLA Modules:
  0.0 115.1 jit_solution(17992537242973750416)
XLA Ops:
  0.6 2.2 %faces.1 = (f32[1,4,16,16,128]{4,3,2,1,0:T(8,128)}, f32[2,1,16,16,128]{4,3,2,1,0:T(8,128)}, f32[1,4,16,128]{3,2,1,0:T(8,128)}, f32[1,4,16,128]{3,2,1,0:T(8,128)}...) custom-call(f32[1024,128]{1,0:T(8,128)} %bitcast.18), custom_call_target="tpu_custom_call" | custom-call | tf_op jit(solution)/shard_map/faces/pallas_call | solution.py:387
  2.8 2.0 %collective-permute-start = (f32[2,1,16,16,128]{4,3,2,1,0:T(8,128)}, f32[2,1,16,16,128]{4,3,2,1,0:T(8,128)S(1)}, u32[]{:S(2)}, u32[]{:S(2)}) collective-permute-start(f32[2,1,16,16,128]{4,3,2,1,0:T(8,128)} %get-tuple-element.31), channel_id=1, source_target_pairs={{0,16},{16,0},{1,17},{17,1},{2,18},{18,2},{3,19},{19,3},{4,20},{20... | collective-permute-start | bytes 786440 | tf_op jit(solution)/shard_map/ppermute | solution.py:103
  4.8 1.3 %collective-permute-start.1 = (f32[1,4,16,128]{3,2,1,0:T(8,128)}, f32[1,4,16,128]{3,2,1,0:T(8,128)S(1)}, u32[]{:S(2)}, u32[]{:S(2)}) collective-permute-start(f32[1,4,16,128]{3,2,1,0:T(8,128)} %get-tuple-element.32), channel_id=1, source_target_pairs={{0,4},{4,8},{8,12},{12,0},{1,5},{5,9},{9,13},{13,1},{2,6},{6,10},{... | collective-permute-start | bytes 98312 | tf_op jit(solution)/shard_map/ppermute | solution.py:109
  6.1 2.0 %collective-permute-start.2 = (f32[1,4,16,128]{3,2,1,0:T(8,128)}, f32[1,4,16,128]{3,2,1,0:T(8,128)S(1)}, u32[]{:S(2)}, u32[]{:S(2)}) collective-permute-start(f32[1,4,16,128]{3,2,1,0:T(8,128)} %get-tuple-element.33), channel_id=1, source_target_pairs={{4,0},{8,4},{12,8},{0,12},{5,1},{9,5},{13,9},{1,13},{6,2},{10,6},{... | collective-permute-start | bytes 98312 | tf_op jit(solution)/shard_map/ppermute | solution.py:110
  8.1 4.2 %collective-permute-start.4 = (f32[2,1,16,128]{3,2,1,0:T(8,128)}, f32[2,1,16,128]{3,2,1,0:T(8,128)S(1)}, u32[]{:S(2)}, u32[]{:S(2)}) collective-permute-start(f32[2,1,16,128]{3,2,1,0:T(8,128)} %get-tuple-element.35), channel_id=1, source_target_pairs={{4,16},{8,20},{12,24},{0,28},{20,0},{24,4},{28,8},{16,12},{5,17},{... | collective-permute-start | bytes 49160 | tf_op jit(solution)/shard_map/ppermute | solution.py:103
  12.3 1.1 copy.19
  13.4 0.2 reshape.29
  13.6 0.1 collective-permute-done.3.xy_low
  13.6 0.0 collective-permute-done.4.xy_high
  13.6 0.0 collective-permute-done.1.y_low
  13.7 0.0 collective-permute-done.2.y_high
  13.7 0.0 copy-start.12
  13.7 0.5 copy-done.13
  14.2 0.0 copy-done.11
  14.3 0.0 copy-done.12
  14.3 0.1 copy-done.3
  14.4 2.3 %pad_faces.2 = (f32[1,112,16,128]{3,2,1,0:T(8,128)}, f32[16,128]{1,0:T(8,128)}, f32[16,128]{1,0:T(8,128)}) custom-call(f32[1,4,16,16,128]{4,3,2,1,0:T(8,128)} %get-tuple-element.30.grid, f32[2,1,16,16,128]{4,3,2,1,0:T(8,128)} %copy-done.3, f32[1,4,16,128]{3,2,1,0:T(8,128)} %copy-done.11, f32[1,4,16,128]{3,2,1,0:T(8,128)} %copy-done.12, ...), custom_call_target="tpu_custom_call" | custom-call | tf_op jit(solution)/shard_map/pad_faces/pallas_call | solution.py:116
  16.7 3.7 %collective-permute-start.5 = (f32[16,128]{1,0:T(8,128)}, f32[16,128]{1,0:T(8,128)S(1)}, u32[]{:S(2)}, u32[]{:S(2)}) collective-permute-start(f32[16,128]{1,0:T(8,128)} %get-tuple-element.37), channel_id=1, source_target_pairs={{0,1},{1,2},{2,3},{3,0},{4,5},{5,6},{6,7},{7,4},{8,9},{9,10},{10,1... | collective-permute-start | bytes 24584 | tf_op jit(solution)/shard_map/ppermute | solution.py:125
  20.4 0.6 pad_maximum_fusion.both
  21.0 0.4 collective-permute-done.5.before
  21.4 2.3 %collective-permute-done.6.after = f32[16,128]{1,0:T(8,128)S(1)} collective-permute-done((f32[16,128]{1,0:T(8,128)}, f32[16,128]{1,0:T(8,128)S(1)}, u32[]{:S(2)}, u32[]{:S(2)}) %collective-permute-start.6) | collective-permute-done | bytes 8224 | tf_op jit(solution)/shard_map/ppermute | solution.py:126
  23.7 0.6 copy-done.18
  24.3 11.6 %conv.1 = (f32[4,16,16,128]{3,2,1,0:T(8,128)}, bf16[112,48,128]{2,1,0:T(8,128)(2,1)}, bf16[112,48,128]{2,1,0:T(8,128)(2,1)}, f32[32,128]{1,0:T(8,128)}) custom-call(f32[1,112,16,128]{3,2,1,0:T(8,128)} %get-tuple-element.36.padded, f32[16,128]{1,0:T(8,128)} %copy-done.17, f32[16,128]{1,0:T(8,128)} %copy-done.18, bf16[32,432]{1,0:T(8,128)(2,1)} %pad_maximum_fusion.both, ...), custom_call_target="tpu_custom_call" | custom-call | tf_op jit(solution)/shard_map/conv/pallas_call | solution.py:395
  35.9 4.9 %all-to-all-start = ((f32[32,1,128]{2,1,0:T(1,128)}), f32[32,1,128]{2,1,0:T(1,128)S(1)}, u32[]{:S(2)}, u32[]{:S(2)}) async-start(f32[32,1,128]{2,1,0:T(1,128)} %bitcast.22), calls=%async_computation | async-start | bytes 32768 | tf_op jit(solution)/shard_map/all_to_all | solution.py:405
  40.9 0.7 copy.21.gamma
  41.5 0.7 copy.22.beta
  42.2 5.4 %all-to-all-done = f32[32,1,128]{2,1,0:T(1,128)S(1)} async-done(((f32[32,1,128]{2,1,0:T(1,128)}), f32[32,1,128]{2,1,0:T(1,128)S(1)}, u32[]{:S(2)}, u32[]{:S(2)}) %all-to-all-start) | async-done | bytes 16416 | tf_op jit(solution)/shard_map/all_to_all | solution.py:405
  47.6 0.6 copy-done.8
  48.2 10.0 %act.1 = (f32[2,4,16,16,128]{4,3,2,1,0:T(8,128)}, f32[2,2,16,16,128]{4,3,2,1,0:T(8,128)}, f32[2,4,16,128]{3,2,1,0:T(8,128)}, f32[2,4,16,128]{3,2,1,0:T(8,128)}, ...) custom-call(f32[4,16,16,128]{3,2,1,0:T(8,128)} %get-tuple-element.39.conv, ...), custom_call_target="tpu_custom_call" | custom-call | tf_op jit(solution)/shard_map/act/pallas_call | solution.py:406
  58.2 0.0 copy-start.21
  58.2 0.7 collective-permute-start.14
  59.0 1.1 collective-permute-done.14
  60.1 0.9 add.15
  60.9 0.3 collective-permute-start.15
  61.2 0.3 collective-permute-start.7
  61.5 2.6 %collective-permute-done.15 = f32[32,512]{1,0:T(8,128)S(1)} collective-permute-done((f32[32,512]{1,0:T(8,128)S(1)}, f32[32,512]{1,0:T(8,128)S(1)}, u32[]{:S(2)}, u32[]{:S(2)}) %collective-permute-start.15) | collective-permute-done | bytes 65568 | tf_op jit(solution)/shard_map/ppermute | solution.py:365
  64.1 0.4 collective-permute-start.16
  64.5 11.2 %collective-permute-done.16 = f32[32,512]{1,0:T(8,128)S(1)} collective-permute-done((f32[32,512]{1,0:T(8,128)S(1)}, f32[32,512]{1,0:T(8,128)S(1)}, u32[]{:S(2)}, u32[]{:S(2)}) %collective-permute-start.16) | collective-permute-done | bytes 65568 | tf_op jit(solution)/shard_map/ppermute | solution.py:365
  75.7 0.4 collective-permute-start.17
  76.2 0.1 copy.25
  76.3 2.6 %collective-permute-done.17 = f32[32,512]{1,0:T(8,128)S(1)} collective-permute-done((f32[32,512]{1,0:T(8,128)S(1)}, f32[32,512]{1,0:T(8,128)S(1)}, u32[]{:S(2)}, u32[]{:S(2)}) %collective-permute-start.17) | collective-permute-done | bytes 65568 | tf_op jit(solution)/shard_map/ppermute | solution.py:365
  78.9 0.4 collective-permute-start.18
  79.3 0.3 collective-permute-start.8
  79.6 3.0 %collective-permute-start.9 = (f32[2,4,16,128]{3,2,1,0:T(8,128)S(1)}, f32[2,4,16,128]{3,2,1,0:T(8,128)S(1)}, u32[]{:S(2)}, u32[]{:S(2)}) collective-permute-start(f32[2,4,16,128]{3,2,1,0:T(8,128)S(1)} %copy-done.21), channel_id=1, source_target_pairs={{4,0},{8,4},{12,8},{0,12},{5,1},{9,5},{13,9},{1,13},{6,2},{10,6},{... | collective-permute-start | bytes 196616 | tf_op jit(solution)/shard_map/ppermute | solution.py:110
  82.6 1.9 %collective-permute-done.18 = f32[32,512]{1,0:T(8,128)S(1)} collective-permute-done((f32[32,512]{1,0:T(8,128)S(1)}, f32[32,512]{1,0:T(8,128)S(1)}, u32[]{:S(2)}, u32[]{:S(2)}) %collective-permute-start.18) | collective-permute-done | bytes 65568 | tf_op jit(solution)/shard_map/ppermute | solution.py:365
  84.5 2.3 %collective-permute-start.11 = (f32[2,2,16,128]{3,2,1,0:T(8,128)S(1)}, f32[2,2,16,128]{3,2,1,0:T(8,128)S(1)}, u32[]{:S(2)}, u32[]{:S(2)}) collective-permute-start(f32[2,2,16,128]{3,2,1,0:T(8,128)S(1)} %copy-done.23), channel_id=1, source_target_pairs={{4,16},{8,20},{12,24},{0,28},{20,0},{24,4},{28,8},{16,12},{5,17},{... | collective-permute-start | bytes 98312 | tf_op jit(solution)/shard_map/ppermute | solution.py:103
  86.8 0.6 pad_maximum_fusion.1.both
  87.4 1.0 collective-permute-done.10.xy_low
  88.4 0.3 collective-permute-done.11.xy_high
  88.8 0.0 copy-start.1
  88.8 0.3 copy-done.9
  89.0 0.3 copy-done.10
  89.3 0.0 copy-done.6
  89.4 0.0 copy-done.7
  89.4 0.2 copy-done.1
  89.6 3.1 %pad_faces.3 = (f32[2,112,16,128]{3,2,1,0:T(8,128)}, f32[32,128]{1,0:T(8,128)}, f32[32,128]{1,0:T(8,128)}) custom-call(f32[2,4,16,16,128]{4,3,2,1,0:T(8,128)} %get-tuple-element.43.grid, f32[2,2,16,16,128]{4,3,2,1,0:T(8,128)} %copy-done.1, f32[2,4,16,128]{3,2,1,0:T(8,128)} %copy-done.6, f32[2,4,16,128]{3,2,1,0:T(8,128)} %copy-done.7, ...), custom_call_target="tpu_custom_call" | custom-call | tf_op jit(solution)/shard_map/pad_faces/pallas_call | solution.py:116
  92.7 5.8 %collective-permute-start.12 = (f32[32,128]{1,0:T(8,128)}, f32[32,128]{1,0:T(8,128)S(1)}, u32[]{:S(2)}, u32[]{:S(2)}) collective-permute-start(f32[32,128]{1,0:T(8,128)} %get-tuple-element.50), channel_id=1, source_target_pairs={{0,1},{1,2},{2,3},{3,0},{4,5},{5,6},{6,7},{7,4},{8,9},{9,10},{10,1... | collective-permute-start | bytes 49160 | tf_op jit(solution)/shard_map/ppermute | solution.py:125
  98.4 0.7 slice_reduce_fusion
  99.1 0.4 collective-permute-done.12.before
  99.5 2.3 %collective-permute-done.13.after = f32[32,128]{1,0:T(8,128)S(1)} collective-permute-done((f32[32,128]{1,0:T(8,128)}, f32[32,128]{1,0:T(8,128)S(1)}, u32[]{:S(2)}, u32[]{:S(2)}) %collective-permute-start.13) | collective-permute-done | bytes 16416 | tf_op jit(solution)/shard_map/ppermute | solution.py:126
  101.8 0.6 copy-done.16
  102.4 11.1 %grads.1 = (f32[1024,128]{1,0:T(8,128)}, f32[16,512]{1,0:T(8,128)}) custom-call(f32[2,112,16,128]{3,2,1,0:T(8,128)} %get-tuple-element.49.padded, f32[32,128]{1,0:T(8,128)} %copy-done.15, f32[32,128]{1,0:T(8,128)} %copy-done.16, f32[32,512]{1,0:T(8,128)} %copy-done.2, f32[16,128]{1,0:T(8,128)} %get-tuple-element.53.scales, ...), custom_call_target="tpu_custom_call" | custom-call | tf_op jit(solution)/shard_map/grads/pallas_call | solution.py:413
  113.5 0.9 reshape.33
  114.4 0.7 copy.24
  (50 shorter events, 0.2 us)
Async XLA Ops:
  2.8 10.9 %collective-permute-start = (f32[2,1,16,16,128]{4,3,2,1,0:T(8,128)}, f32[2,1,16,16,128]{4,3,2,1,0:T(8,128)S(1)}, u32[]{:S(2)}, u32[]{:S(2)}) collective-permute-start(f32[2,1,16,16,128]{4,3,2,1,0:T(8,128)} %get-tuple-element.31), channel_id=1, source_target_pairs={{0,16},{16,0},{1,17},{17,1},{2,18},{18,2},{3,19},{19,3},{4,20},{20... | collective-permute-start | bytes 786440 | tf_op jit(solution)/shard_map/ppermute | solution.py:103
  4.8 8.8 %collective-permute-start.1 = (f32[1,4,16,128]{3,2,1,0:T(8,128)}, f32[1,4,16,128]{3,2,1,0:T(8,128)S(1)}, u32[]{:S(2)}, u32[]{:S(2)}) collective-permute-start(f32[1,4,16,128]{3,2,1,0:T(8,128)} %get-tuple-element.32), channel_id=1, source_target_pairs={{0,4},{4,8},{8,12},{12,0},{1,5},{5,9},{9,13},{13,1},{2,6},{6,10},{... | collective-permute-start | bytes 98312 | tf_op jit(solution)/shard_map/ppermute | solution.py:109
  6.1 7.6 %collective-permute-start.2 = (f32[1,4,16,128]{3,2,1,0:T(8,128)}, f32[1,4,16,128]{3,2,1,0:T(8,128)S(1)}, u32[]{:S(2)}, u32[]{:S(2)}) collective-permute-start(f32[1,4,16,128]{3,2,1,0:T(8,128)} %get-tuple-element.33), channel_id=1, source_target_pairs={{4,0},{8,4},{12,8},{0,12},{5,1},{9,5},{13,9},{1,13},{6,2},{10,6},{... | collective-permute-start | bytes 98312 | tf_op jit(solution)/shard_map/ppermute | solution.py:110
  8.1 5.5 %collective-permute-start.3 = (f32[2,1,16,128]{3,2,1,0:T(8,128)}, f32[2,1,16,128]{3,2,1,0:T(8,128)S(1)}, u32[]{:S(2)}, u32[]{:S(2)}) collective-permute-start(f32[2,1,16,128]{3,2,1,0:T(8,128)} %get-tuple-element.34), channel_id=1, source_target_pairs={{0,20},{4,24},{8,28},{12,16},{16,4},{20,8},{24,12},{28,0},{1,21},{... | collective-permute-start | bytes 49160 | tf_op jit(solution)/shard_map/ppermute | solution.py:103
  8.1 5.5 %collective-permute-start.4 = (f32[2,1,16,128]{3,2,1,0:T(8,128)}, f32[2,1,16,128]{3,2,1,0:T(8,128)S(1)}, u32[]{:S(2)}, u32[]{:S(2)}) collective-permute-start(f32[2,1,16,128]{3,2,1,0:T(8,128)} %get-tuple-element.35), channel_id=1, source_target_pairs={{4,16},{8,20},{12,24},{0,28},{20,0},{24,4},{28,8},{16,12},{5,17},{... | collective-permute-start | bytes 49160 | tf_op jit(solution)/shard_map/ppermute | solution.py:103
  12.3 28.5 %copy-start.19 = (f32[16]{0:T(128)S(1)}, f32[16]{0:T(128)}, u32[]{:S(2)}) copy-start(f32[16]{0:T(128)} %param.7) | copy-start | bytes 196
  12.3 29.2 %copy-start.20 = (f32[16]{0:T(128)S(1)}, f32[16]{0:T(128)}, u32[]{:S(2)}) copy-start(f32[16]{0:T(128)} %param.8) | copy-start | bytes 196
  13.6 10.1 %copy-start.5 = (bf16[16,432]{1,0:T(8,128)(2,1)}, bf16[16,432]{1,0:T(8,128)(2,1)S(1)}, u32[]{:S(2)}) copy-start(bf16[16,432]{1,0:T(8,128)(2,1)S(1)} %get-tuple-element.68.top) | copy-start | bytes 41476
  13.6 0.6 copy-start.13
  13.6 0.6 copy-start.14
  13.6 0.6 copy-start.11
  13.7 0.6 copy-start.12
  13.7 0.7 copy-start.3
  16.7 4.7 %collective-permute-start.5 = (f32[16,128]{1,0:T(8,128)}, f32[16,128]{1,0:T(8,128)S(1)}, u32[]{:S(2)}, u32[]{:S(2)}) collective-permute-start(f32[16,128]{1,0:T(8,128)} %get-tuple-element.37), channel_id=1, source_target_pairs={{0,1},{1,2},{2,3},{3,0},{4,5},{5,6},{6,7},{7,4},{8,9},{9,10},{10,1... | collective-permute-start | bytes 24584 | tf_op jit(solution)/shard_map/ppermute | solution.py:125
  20.4 3.3 %collective-permute-start.6 = (f32[16,128]{1,0:T(8,128)}, f32[16,128]{1,0:T(8,128)S(1)}, u32[]{:S(2)}, u32[]{:S(2)}) collective-permute-start(f32[16,128]{1,0:T(8,128)} %get-tuple-element.38), channel_id=1, source_target_pairs={{1,0},{2,1},{3,2},{0,3},{5,4},{6,5},{7,6},{4,7},{9,8},{10,9},{11,1... | collective-permute-start | bytes 24584 | tf_op jit(solution)/shard_map/ppermute | solution.py:126
  21.4 2.3 %copy-start.17 = (f32[16,128]{1,0:T(8,128)}, f32[16,128]{1,0:T(8,128)S(1)}, u32[]{:S(2)}) copy-start(f32[16,128]{1,0:T(8,128)S(1)} %collective-permute-done.5.before) | copy-start | bytes 24580
  23.7 0.6 copy-start.18
  35.9 11.7 %all-to-all-start = ((f32[32,1,128]{2,1,0:T(1,128)}), f32[32,1,128]{2,1,0:T(1,128)S(1)}, u32[]{:S(2)}, u32[]{:S(2)}) async-start(f32[32,1,128]{2,1,0:T(1,128)} %bitcast.22), calls=%async_computation | async-start | bytes 32768 | tf_op jit(solution)/shard_map/all_to_all | solution.py:405
  47.6 0.6 copy-start.8
  48.2 27.9 %copy-start = (f32[16,16,3,3,3]{1,0,4,3,2:T(8,128)S(1)}, f32[16,16,3,3,3]{1,0,4,3,2:T(8,128)}, u32[]{:S(2)}) copy-start(f32[16,16,3,3,3]{1,0,4,3,2:T(8,128)} %param.6) | copy-start | bytes 82948
  58.2 21.1 %copy-start.22 = (f32[2,4,16,128]{3,2,1,0:T(8,128)S(1)}, f32[2,4,16,128]{3,2,1,0:T(8,128)}, u32[]{:S(2)}) copy-start(f32[2,4,16,128]{3,2,1,0:T(8,128)} %get-tuple-element.45) | copy-start | bytes 196612
  58.2 21.4 %copy-start.21 = (f32[2,4,16,128]{3,2,1,0:T(8,128)S(1)}, f32[2,4,16,128]{3,2,1,0:T(8,128)}, u32[]{:S(2)}) copy-start(f32[2,4,16,128]{3,2,1,0:T(8,128)} %get-tuple-element.46) | copy-start | bytes 196612
  58.2 24.4 %copy-start.24 = (f32[2,2,16,128]{3,2,1,0:T(8,128)S(1)}, f32[2,2,16,128]{3,2,1,0:T(8,128)}, u32[]{:S(2)}) copy-start(f32[2,2,16,128]{3,2,1,0:T(8,128)} %get-tuple-element.47) | copy-start | bytes 98308
  58.2 26.3 %copy-start.23 = (f32[2,2,16,128]{3,2,1,0:T(8,128)S(1)}, f32[2,2,16,128]{3,2,1,0:T(8,128)}, u32[]{:S(2)}) copy-start(f32[2,2,16,128]{3,2,1,0:T(8,128)} %get-tuple-element.48) | copy-start | bytes 98308
  58.2 1.8 %collective-permute-start.14 = (f32[32,512]{1,0:T(8,128)}, f32[32,512]{1,0:T(8,128)S(1)}, u32[]{:S(2)}, u32[]{:S(2)}) collective-permute-start(f32[32,512]{1,0:T(8,128)} %get-tuple-element.52), channel_id=1, source_target_pairs={{0,1},{1,0},{2,3},{3,2},{4,5},{5,4},{6,7},{7,6},{8,9},{9,8},{10,11... | collective-permute-start | bytes 196616 | tf_op jit(solution)/shard_map/ppermute | solution.py:365
  60.9 3.2 %collective-permute-start.15 = (f32[32,512]{1,0:T(8,128)S(1)}, f32[32,512]{1,0:T(8,128)S(1)}, u32[]{:S(2)}, u32[]{:S(2)}) collective-permute-start(f32[32,512]{1,0:T(8,128)S(1)} %add.15), channel_id=1, source_target_pairs={{0,2},{1,3},{2,0},{3,1},{4,6},{5,7},{6,4},{7,5},{8,10},{9,11},{10,... | collective-permute-start | bytes 196616 | tf_op jit(solution)/shard_map/ppermute | solution.py:365
  61.2 27.5 %collective-permute-start.7 = (f32[2,2,16,16,128]{4,3,2,1,0:T(8,128)}, f32[2,2,16,16,128]{4,3,2,1,0:T(8,128)S(1)}, u32[]{:S(2)}, u32[]{:S(2)}) collective-permute-start(f32[2,2,16,16,128]{4,3,2,1,0:T(8,128)} %get-tuple-element.44), channel_id=1, source_target_pairs={{0,16},{16,0},{1,17},{17,1},{2,18},{18,2},{3,19},{19,3},{4,20},{20... | collective-permute-start | bytes 1572872 | tf_op jit(solution)/shard_map/ppermute | solution.py:103
  64.1 11.6 %collective-permute-start.16 = (f32[32,512]{1,0:T(8,128)S(1)}, f32[32,512]{1,0:T(8,128)S(1)}, u32[]{:S(2)}, u32[]{:S(2)}) collective-permute-start(f32[32,512]{1,0:T(8,128)S(1)} %add.16), channel_id=1, source_target_pairs={{0,16},{16,0},{1,17},{17,1},{2,18},{18,2},{3,19},{19,3},{4,20},{20... | collective-permute-start | bytes 196616 | tf_op jit(solution)/shard_map/ppermute | solution.py:365
  75.7 3.2 %collective-permute-start.17 = (f32[32,512]{1,0:T(8,128)S(1)}, f32[32,512]{1,0:T(8,128)S(1)}, u32[]{:S(2)}, u32[]{:S(2)}) collective-permute-start(f32[32,512]{1,0:T(8,128)S(1)} %add.17), channel_id=1, source_target_pairs={{0,4},{4,0},{8,12},{12,8},{1,5},{5,1},{9,13},{13,9},{2,6},{6,2},{1... | collective-permute-start | bytes 196616 | tf_op jit(solution)/shard_map/ppermute | solution.py:365
  78.9 5.6 %collective-permute-start.18 = (f32[32,512]{1,0:T(8,128)S(1)}, f32[32,512]{1,0:T(8,128)S(1)}, u32[]{:S(2)}, u32[]{:S(2)}) collective-permute-start(f32[32,512]{1,0:T(8,128)S(1)} %add.18), channel_id=1, source_target_pairs={{0,8},{4,12},{8,0},{12,4},{1,9},{5,13},{9,1},{13,5},{2,10},{6,14},... | collective-permute-start | bytes 196616 | tf_op jit(solution)/shard_map/ppermute | solution.py:365
  79.3 22.5 %copy-start.4 = (bf16[16,432]{1,0:T(8,128)(2,1)}, bf16[16,432]{1,0:T(8,128)(2,1)S(1)}, u32[]{:S(2)}) copy-start(bf16[16,432]{1,0:T(8,128)(2,1)S(1)} %get-tuple-element.66.top) | copy-start | bytes 41476
  79.3 9.4 %collective-permute-start.8 = (f32[2,4,16,128]{3,2,1,0:T(8,128)S(1)}, f32[2,4,16,128]{3,2,1,0:T(8,128)S(1)}, u32[]{:S(2)}, u32[]{:S(2)}) collective-permute-start(f32[2,4,16,128]{3,2,1,0:T(8,128)S(1)} %copy-done.22), channel_id=1, source_target_pairs={{0,4},{4,8},{8,12},{12,0},{1,5},{5,9},{9,13},{13,1},{2,6},{6,10},{... | collective-permute-start | bytes 196616 | tf_op jit(solution)/shard_map/ppermute | solution.py:109
  79.6 9.1 %collective-permute-start.9 = (f32[2,4,16,128]{3,2,1,0:T(8,128)S(1)}, f32[2,4,16,128]{3,2,1,0:T(8,128)S(1)}, u32[]{:S(2)}, u32[]{:S(2)}) collective-permute-start(f32[2,4,16,128]{3,2,1,0:T(8,128)S(1)} %copy-done.21), channel_id=1, source_target_pairs={{4,0},{8,4},{12,8},{0,12},{5,1},{9,5},{13,9},{1,13},{6,2},{10,6},{... | collective-permute-start | bytes 196616 | tf_op jit(solution)/shard_map/ppermute | solution.py:110
  82.6 5.8 %collective-permute-start.10 = (f32[2,2,16,128]{3,2,1,0:T(8,128)S(1)}, f32[2,2,16,128]{3,2,1,0:T(8,128)S(1)}, u32[]{:S(2)}, u32[]{:S(2)}) collective-permute-start(f32[2,2,16,128]{3,2,1,0:T(8,128)S(1)} %copy-done.24), channel_id=1, source_target_pairs={{0,20},{4,24},{8,28},{12,16},{16,4},{20,8},{24,12},{28,0},{1,21},{... | collective-permute-start | bytes 98312 | tf_op jit(solution)/shard_map/ppermute | solution.py:103
  84.5 4.2 %collective-permute-start.11 = (f32[2,2,16,128]{3,2,1,0:T(8,128)S(1)}, f32[2,2,16,128]{3,2,1,0:T(8,128)S(1)}, u32[]{:S(2)}, u32[]{:S(2)}) collective-permute-start(f32[2,2,16,128]{3,2,1,0:T(8,128)S(1)} %copy-done.23), channel_id=1, source_target_pairs={{4,16},{8,20},{12,24},{0,28},{20,0},{24,4},{28,8},{16,12},{5,17},{... | collective-permute-start | bytes 98312 | tf_op jit(solution)/shard_map/ppermute | solution.py:103
  87.4 14.4 %copy-start.2 = (f32[32,512]{1,0:T(8,128)}, f32[32,512]{1,0:T(8,128)S(1)}, u32[]{:S(2)}) copy-start(f32[32,512]{1,0:T(8,128)S(1)} %add.19.sums) | copy-start | bytes 196612
  88.4 0.6 copy-start.9
  88.7 0.6 copy-start.10
  88.7 0.6 copy-start.6
  88.7 0.6 copy-start.7
  88.8 0.8 copy-start.1
  92.7 6.9 %collective-permute-start.12 = (f32[32,128]{1,0:T(8,128)}, f32[32,128]{1,0:T(8,128)S(1)}, u32[]{:S(2)}, u32[]{:S(2)}) collective-permute-start(f32[32,128]{1,0:T(8,128)} %get-tuple-element.50), channel_id=1, source_target_pairs={{0,1},{1,2},{2,3},{3,0},{4,5},{5,6},{6,7},{7,4},{8,9},{9,10},{10,1... | collective-permute-start | bytes 49160 | tf_op jit(solution)/shard_map/ppermute | solution.py:125
  98.4 3.4 %collective-permute-start.13 = (f32[32,128]{1,0:T(8,128)}, f32[32,128]{1,0:T(8,128)S(1)}, u32[]{:S(2)}, u32[]{:S(2)}) collective-permute-start(f32[32,128]{1,0:T(8,128)} %get-tuple-element.51), channel_id=1, source_target_pairs={{1,0},{2,1},{3,2},{0,3},{5,4},{6,5},{7,6},{4,7},{9,8},{10,9},{11,1... | collective-permute-start | bytes 49160 | tf_op jit(solution)/shard_map/ppermute | solution.py:126
  99.5 2.3 %copy-start.15 = (f32[32,128]{1,0:T(8,128)}, f32[32,128]{1,0:T(8,128)S(1)}, u32[]{:S(2)}) copy-start(f32[32,128]{1,0:T(8,128)S(1)} %collective-permute-done.12.before) | copy-start | bytes 49156
  101.8 0.6 copy-start.16

commit v2 on v1

--- a/solution.py
+++ b/solution.py
@@ -1,4 +1,5 @@
 import functools
+import math
 
 import jax
 import jax.numpy as jnp
@@ -11,14 +12,22 @@
 F32, BF16 = jnp.float32, jnp.bfloat16
 
 
-def call(body, outs, scratch=(), name=None):
-    return pl.pallas_call(
+def call(body, outs, scratch=(), name=None, last=False):
+    run = pl.pallas_call(
         body,
-        out_shape=[jax.ShapeDtypeStruct(shape, kind) for shape, kind in outs],
+        out_shape=[
+            jax.ShapeDtypeStruct(shape, kind) if last else pltpu.VMEM(shape, kind)
+            for shape, kind in outs
+        ],
         scratch_shapes=list(scratch),
         name=name,
-        compiler_params=pltpu.CompilerParams(vmem_limit_bytes=60 * 2**20),
-    )
+        compiler_params=pltpu.CompilerParams(vmem_limit_bytes=16 * 2**20),
+    )
+
+    def onchip(*args):
+        return run(*[pltpu.with_memory_space_constraint(arg, pltpu.VMEM) for arg in args])
+
+    return onchip
 
 
 def turns(count):
@@ -168,21 +177,22 @@
     return wide_part[:chans] + (wide_part[chans:] + thin_part)
 
 
-def conv_kernel(dims, padded, before, after, both, top, conv, high, low, stats):
-    size_x, size_y, chans, size_z = dims
-    wide = size_y + 2
+def volume_shifts(padded, before, after, high, low):
+    chans, size_z = padded.shape[2:]
     group = 128 // chans
-
-    def shifts(at, _):
+    for at in range(padded.shape[1] // group):
         edges = halo_block(before, after, at, size_z)
         for one in range(group):
             pair = at * group + one
             edge = edges[one * chans : (one + 1) * chans]
             put_shifts(pair, padded[0, pair], edge, high, low)
-        return 0
-
-    lax.fori_loop(0, padded.shape[1] // group, shifts, 0)
-    width = 2
+
+
+def conv_kernel(dims, padded, before, after, both, top, conv, stats, high, low):
+    size_x, size_y, chans, size_z = dims
+    wide = size_y + 2
+    volume_shifts(padded, before, after, high, low)
+    width = math.gcd(size_y, 8)
     both_now, top_now = both[...], top[...]
 
     def step(at, carry):
@@ -197,7 +207,9 @@
         return total, source
 
     zero = jnp.zeros((chans, size_z), F32)
-    total, source = lax.fori_loop(0, size_x * size_y // width, step, (zero, zero))
+    total, source = lax.fori_loop(
+        0, size_x * size_y // width, step, (zero, zero), unroll=True
+    )
     sums = jnp.sum(total, axis=1, keepdims=True)
     centre = sums * (1.0 / (size_x * size_y * size_z))
 
@@ -207,7 +219,7 @@
             squares = squares + away * away
         return squares
 
-    squares = lax.fori_loop(0, size_x, spread, zero)
+    squares = lax.fori_loop(0, size_x, spread, zero, unroll=True)
     lane = lax.broadcasted_iota(jnp.int32, (chans, 128), 1)
     table = jnp.where(
         lane == 0,
@@ -223,9 +235,10 @@
     stats[...] = jnp.broadcast_to(row, stats.shape)
 
 
-def act_kernel(dims, count, conv, cotangent, high, low, stats, gamma, beta, *outs):
-    size_x, size_y, chans, size_z = dims
-    store, sums, scales = outs[:6], outs[6], outs[7]
+def act_kernel(dims, count, conv, cotangent, padded, before, after, stats, gamma, beta, *outs):
+    size_x, size_y, chans, size_z = dims
+    store, sums, scales, high, low = outs[:6], *outs[6:]
+    volume_shifts(padded, before, after, high, low)
     local = float(size_x * size_y * size_z)
     wide = size_y + 2
     rows = stats[...]
@@ -235,11 +248,16 @@
     spread_row = jnp.sum(away * away, axis=0, keepdims=True) * (local / count)
     var_row = mean_row + pltpu.roll(spread_row, chans, 1)
     rstd_row = lax.rsqrt(var_row + 1e-05)
-    table = jnp.concatenate([mean_row, rstd_row, jnp.zeros((126, 128), F32)], axis=0).T
+    blank = jnp.zeros((1, 128 - chans), F32)
+    gain_row = jnp.concatenate([gamma[...], blank], axis=1)
+    shift_row = jnp.concatenate([beta[...], blank], axis=1)
+    table = jnp.concatenate(
+        [mean_row, rstd_row, gain_row, shift_row, jnp.zeros((124, 128), F32)], axis=0
+    ).T
     mean = table[:chans, 0:1]
     rstd = table[chans : 2 * chans, 1:2]
     level = table[2 * chans : 3 * chans, 0:1]
-    gain, shift = gamma[...], beta[...]
+    gain, shift = table[:chans, 2:3], table[:chans, 3:4]
     scales[...] = jnp.broadcast_to(gain * rstd, scales.shape)
     gamma_sum = jnp.zeros((chans, size_z), F32)
     beta_sum = jnp.zeros((chans, size_z), F32)
@@ -290,7 +308,7 @@
 
     taps = 27 * chans
     total = lax.fori_loop(
-        0, size_x * size_y // width, step, jnp.zeros((taps, 5 * chans), F32)
+        0, size_x * size_y // width, step, jnp.zeros((taps, 5 * chans), F32), unroll=True
     )
     tall = -(-taps // 128) * 128
     levels = jnp.concatenate([level] * 27, axis=0)
@@ -309,16 +327,15 @@
     sums[chans : 2 * chans] = other
 
 
-def grad_kernel(dims, count, padded, before, after, sums, scales, both, top, out, weight_grad, high, low):
+def grad_kernel(dims, count, padded, before, after, sums, scales, both, top, out, high, low):
     size_x, size_y, chans, size_z = dims
     wide = size_y + 2
     group = 128 // chans
     taps = 27 * chans
     scale = scales[...]
-    main, other = sums[0:chans], sums[chans : 2 * chans]
+    main = sums[0:chans]
     gamma_mean = main[:, taps : taps + 1] * (1.0 / count)
     beta_mean = main[:, taps + 1 : taps + 2] * (1.0 / count)
-    weight_grad[...] = scale[:, 0:1] * (main - gamma_mean * other)
     gamma_wide = jnp.broadcast_to(gamma_mean, (chans, size_z))
     beta_wide = jnp.broadcast_to(beta_mean, (chans, size_z))
     rows = before.shape[0] // 2
@@ -337,8 +354,8 @@
             put_shifts(pair, value, edge, high, low)
         return 0
 
-    lax.fori_loop(0, padded.shape[1] // group, shifts, 0)
-    width = 2
+    lax.fori_loop(0, padded.shape[1] // group, shifts, 0, unroll=True)
+    width = math.gcd(size_y, 8)
     both_now, top_now = both[...], top[...]
     stride = size_x * size_y
 
@@ -351,7 +368,7 @@
             ]
         return 0
 
-    lax.fori_loop(0, size_x * size_y // width, step, 0)
+    lax.fori_loop(0, size_x * size_y // width, step, 0, unroll=True)
 
 
 def total_over(value):
@@ -392,40 +409,35 @@
     back = weight[:, :, ::-1, ::-1, ::-1].transpose(1, 2, 3, 4, 0).reshape(chans, taps)
     back_both, back_top = two_parts(back)
     pairs = padded.shape[1]
-    conv, high, low, stats = call(
+    shifted = [pltpu.VMEM((pairs, 3 * chans, size_z), BF16)] * 2
+    conv, stats = call(
         functools.partial(conv_kernel, dims),
-        [
-            ((size_x, size_y, chans, size_z), F32),
-            ((pairs, 3 * chans, size_z), BF16),
-            ((pairs, 3 * chans, size_z), BF16),
-            ((devices, 128), F32),
-        ],
+        [((size_x, size_y, chans, size_z), F32), ((devices, 128), F32)],
+        scratch=shifted,
         name="conv",
     )(padded, before, after, both, top)
     stats = lax.all_to_all(stats, AXES, 0, 0, tiled=True)
+    stats, back_both, back_top = lax.optimization_barrier((stats, back_both, back_top))
     *store, sums, scales = call(
         functools.partial(act_kernel, dims, count),
         face_shapes(2, dims) + [((2 * chans, tall), F32), ((chans, size_z), F32)],
+        scratch=shifted,
         name="act",
-    )(conv, cotangent.reshape(flat), high, low, stats, gamma[:, None], beta[:, None])
+    )(conv, cotangent.reshape(flat), padded, before, after, stats, gamma[None], beta[None])
     padded, before, after = exchange(2, dims, *store)
     sums = total_over(sums)
-    input_grad, weight_grad = call(
+    main, other = sums[:chans, :taps], sums[chans:, :taps]
+    gamma_grad, beta_grad = sums[:chans, taps], sums[:chans, taps + 1]
+    weight_grad = scales[:, :1] * (main - (gamma_grad / count)[:, None] * other)
+    weight_grad = weight_grad.reshape(chans, 3, 3, 3, chans).transpose(0, 4, 1, 2, 3)
+    (input_grad,) = call(
         functools.partial(grad_kernel, dims, count),
-        [(flat, F32), ((chans, tall), F32)],
-        scratch=[
-            pltpu.VMEM((pairs, 3 * chans, size_z), BF16),
-            pltpu.VMEM((pairs, 3 * chans, size_z), BF16),
-        ],
+        [(flat, F32)],
+        scratch=shifted,
         name="grads",
+        last=True,
     )(padded, before, after, sums, scales, back_both, back_top)
-    weight_grad = weight_grad[:, :taps].reshape(chans, 3, 3, 3, chans).transpose(0, 4, 1, 2, 3)
-    return (
-        input_grad.reshape(volume.shape),
-        weight_grad,
-        sums[:chans, taps],
-        sums[:chans, taps + 1],
-    )
+    return input_grad.reshape(volume.shape), weight_grad, gamma_grad, beta_grad
 
 
 def solution(mesh):

time: 116 us -> 79.6 us (0.69)
  Pallas kernels: 40.2 us -> 12.5 us
  local copies, waits for them, and re-layouts: 8.37 us -> 4.36 us
  waiting for transfers between devices: 31.6 us -> 29 us
  other arithmetic: 2.14 us -> 0.87 us
    pallas_call x6, Pallas kernels: 40.2 us -> 12.5 us  [onchip(): run(*[pltpu.with_memory_space_constraint(arg, pltpu.VMEM) for arg in args])]
    ppermute x5, waiting for transfers between devices: 19.4 us -> 16.7 us  [total_over(): lax.ppermute(value, axis, [(i, i ^ step) for i in range(count)])]
    unnamed x51 -> x9, local copies, waits for them, and re-layouts: 4.04 us -> 1.75 us
    broadcast_in_dim x2 -> x0, local copies, waits for them, and re-layouts: 1.35 us -> none  [the longest x1 0.68 us: shards(): beta[:, None]]
    all_to_all x1, waiting for transfers between devices: 5.44 us -> 6.71 us  [shards(): stats = lax.all_to_all(stats, AXES, 0, 0, tiled=True)]
    concatenate x2, other arithmetic: 1.23 us -> 0.02 us  [two_parts(): return (jnp.concatenate([top, rest], axis=0), top)]
  transfers between devices with their start and end apart: 20 -> 20, of which waited for: 13 -> 9; matrix products, arithmetic and copies ran while one was open for 4% -> 5% of each run, Pallas kernels for 0% -> 0%
where the time goes in v2:
time: 79.6 us; the launch traced here: 79.3 us
  starting transfers between devices  31.9 us (40%)
  waiting for transfers between devices  29 us (36%)
  Pallas kernels  12.5 us (16%)
  local copies, waits for them, and re-layouts  4.36 us (5%)
  other arithmetic  0.87 us (1%)
    ppermute x5, waiting for transfers between devices, total_over(): lax.ppermute(value, axis, [(i, i ^ step) for i in range(count)])  16.7 us
    pallas_call x6, Pallas kernels, onchip(): run(*[pltpu.with_memory_space_constraint(arg, pltpu.VMEM) for arg in args])  12.5 us
    ppermute x6, starting transfers between devices, over_x(): return lax.ppermute(pieces, axes, pairs(up_x))  9.27 us
    ppermute x2, starting transfers between devices, exchange(): before = lax.ppermute(last, 'gz', up_z)  8.62 us
    all_to_all x1, waiting for transfers between devices, shards(): stats = lax.all_to_all(stats, AXES, 0, 0, tiled=True)  6.71 us
    ppermute x2, waiting for transfers between devices, exchange(): after = lax.ppermute(first, 'gz', down_z)  4.48 us
    all_to_all x1, starting transfers between devices, shards(): stats = lax.all_to_all(stats, AXES, 0, 0, tiled=True)  4.25 us
    ppermute x2, starting transfers between devices, exchange(): high = lax.ppermute(y_low, 'gy', down_y)  4.03 us
  transfers between devices with their start and end apart: 20, of which 9 were waited for; matrix products, arithmetic and copies ran while one was open for 5% of the time, Pallas kernels for 0%

profile of v2, /device:TPU:1, one launch (start us, length us, event | category | flops | bytes accessed | tf_op | source)
XLA Modules:
  0.0 79.3 jit_solution(17544269375984732782)
XLA Ops:
  0.6 0.0 copy-start.1
  0.6 1.0 %copy-done.1 = f32[16,4,16,128]{3,2,1,0:T(8,128)S(1)} copy-done((f32[16,4,16,128]{3,2,1,0:T(8,128)S(1)}, f32[16,4,16,128]{3,2,1,0:T(8,128)}, u32[]{:S(2)}) %copy-start.1) | copy-done | bytes 524312
  1.7 0.3 faces.1
  2.0 2.1 %collective-permute-start = (f32[2,1,16,16,128]{4,3,2,1,0:T(8,128)S(1)}, f32[2,1,16,16,128]{4,3,2,1,0:T(8,128)S(1)}, u32[]{:S(2)}, u32[]{:S(2)}) collective-permute-start(f32[2,1,16,16,128]{4,3,2,1,0:T(8,128)S(1)} %get-tuple-element.30), channel_id=1, source_target_pairs={{0,16},{16,0},{1,17},{17,1},{2,18},{18,2},{3,19},{19,3},{4,20},{20... | collective-permute-start | bytes 786440 | tf_op jit(solution)/shard_map/ppermute | solution.py:112
  4.1 1.3 %collective-permute-start.1 = (f32[1,4,16,128]{3,2,1,0:T(8,128)S(1)}, f32[1,4,16,128]{3,2,1,0:T(8,128)S(1)}, u32[]{:S(2)}, u32[]{:S(2)}) collective-permute-start(f32[1,4,16,128]{3,2,1,0:T(8,128)S(1)} %get-tuple-element.31), channel_id=1, source_target_pairs={{0,4},{4,8},{8,12},{12,0},{1,5},{5,9},{9,13},{13,1},{2,6},{6,10},{... | collective-permute-start | bytes 98312 | tf_op jit(solution)/shard_map/ppermute | solution.py:118
  5.4 2.0 %collective-permute-start.2 = (f32[1,4,16,128]{3,2,1,0:T(8,128)S(1)}, f32[1,4,16,128]{3,2,1,0:T(8,128)S(1)}, u32[]{:S(2)}, u32[]{:S(2)}) collective-permute-start(f32[1,4,16,128]{3,2,1,0:T(8,128)S(1)} %get-tuple-element.32), channel_id=1, source_target_pairs={{4,0},{8,4},{12,8},{0,12},{5,1},{9,5},{13,9},{1,13},{6,2},{10,6},{... | collective-permute-start | bytes 98312 | tf_op jit(solution)/shard_map/ppermute | solution.py:119
  7.4 0.0 collective-permute-start.3
  7.4 4.2 %collective-permute-start.4 = (f32[2,1,16,128]{3,2,1,0:T(8,128)S(1)}, f32[2,1,16,128]{3,2,1,0:T(8,128)S(1)}, u32[]{:S(2)}, u32[]{:S(2)}) collective-permute-start(f32[2,1,16,128]{3,2,1,0:T(8,128)S(1)} %get-tuple-element.34), channel_id=1, source_target_pairs={{4,16},{8,20},{12,24},{0,28},{20,0},{24,4},{28,8},{16,12},{5,17},{... | collective-permute-start | bytes 49160 | tf_op jit(solution)/shard_map/ppermute | solution.py:112
  11.6 0.0 copy-start
  11.6 0.0 copy-start.2
  11.6 0.0 copy-start.3
  11.6 1.1 %copy.15 = f32[16,3,3,3,16]{4,3,2,1,0:T(4,128)S(1)} copy(f32[16,3,3,3,16]{4,0,3,2,1:T(8,128)} %bitcast.20) | data formatting | bytes 55296 | tf_op jit(solution)/shard_map/transpose | solution.py:408
  12.7 0.2 reshape.29
  12.9 1.0 %rev.3 = f32[16,16,3,3,3]{1,0,4,3,2:T(8,128)S(1)} reverse(f32[16,16,3,3,3]{1,0,4,3,2:T(8,128)} %param.6), dimensions={2,3,4} | reverse | bytes 55296 | tf_op jit(solution)/shard_map/rev | solution.py:409
  13.8 0.1 copy.19
  13.9 0.0 collective-permute-done.3.xy_low
  13.9 0.0 collective-permute-done.4.xy_high
  14.0 0.0 collective-permute-done.1.y_low
  14.0 0.0 collective-permute-done.2.y_high
  14.0 0.0 collective-permute-done.x_face
  14.0 0.3 pad_faces.2
  14.3 3.2 %collective-permute-start.5 = (f32[16,128]{1,0:T(8,128)S(1)}, f32[16,128]{1,0:T(8,128)S(1)}, u32[]{:S(2)}, u32[]{:S(2)}) collective-permute-start(f32[16,128]{1,0:T(8,128)S(1)} %get-tuple-element.36), channel_id=1, source_target_pairs={{0,1},{1,2},{2,3},{3,0},{4,5},{5,6},{6,7},{7,4},{8,9},{9,10},{10,1... | collective-permute-start | bytes 24584 | tf_op jit(solution)/shard_map/ppermute | solution.py:134
  17.5 0.0 collective-permute-start.6
  17.5 0.8 collective-permute-done.5.before
  18.3 2.3 %collective-permute-done.6.after = f32[16,128]{1,0:T(8,128)S(1)} collective-permute-done((f32[16,128]{1,0:T(8,128)S(1)}, f32[16,128]{1,0:T(8,128)S(1)}, u32[]{:S(2)}, u32[]{:S(2)}) %collective-permute-start.6) | collective-permute-done | bytes 8224 | tf_op jit(solution)/shard_map/ppermute | solution.py:135
  20.6 3.3 %conv.1 = (f32[4,16,16,128]{3,2,1,0:T(8,128)S(1)}, f32[32,128]{1,0:T(8,128)}) custom-call(f32[1,112,16,128]{3,2,1,0:T(8,128)S(1)} %get-tuple-element.35.padded, f32[16,128]{1,0:T(8,128)S(1)} %collective-permute-done.5.before, f32[16,128]{1,0:T(8,128)S(1)} %collective-permute-done.6.after, bf16[32,432]{1,0:T(8,128)(2,1)S(1)} %pad_maximum_fusion.both, ...), custom_call_target="tpu_custom_call" | custom-call | tf_op jit(solution)/shard_map/conv/pallas_call | solution.py:28
  23.8 4.3 %all-to-all-start = ((f32[32,1,128]{2,1,0:T(1,128)}), f32[32,1,128]{2,1,0:T(1,128)S(1)}, u32[]{:S(2)}, u32[]{:S(2)}) async-start(f32[32,1,128]{2,1,0:T(1,128)} %bitcast.4), calls=%async_computation | async-start | bytes 32768 | tf_op jit(solution)/shard_map/all_to_all | solution.py:419
  28.1 6.7 %all-to-all-done = f32[32,1,128]{2,1,0:T(1,128)S(1)} async-done(((f32[32,1,128]{2,1,0:T(1,128)}), f32[32,1,128]{2,1,0:T(1,128)S(1)}, u32[]{:S(2)}, u32[]{:S(2)}) %all-to-all-start) | async-done | bytes 16416 | tf_op jit(solution)/shard_map/all_to_all | solution.py:419
  34.8 0.0 copy-done
  34.8 0.0 copy-done.2
  34.8 0.0 copy-done.3
  34.8 4.8 %act.1 = (f32[2,4,16,16,128]{4,3,2,1,0:T(8,128)S(1)}, f32[2,2,16,16,128]{4,3,2,1,0:T(8,128)S(1)}, f32[2,4,16,128]{3,2,1,0:T(8,128)S(1)}, f32[2,4,16,128]{3,2,1,0...) custom-call(f32[4,16,16,128]{3,2,1,0:T(8,128)S(1)} %get-tuple-elemen, ...), custom_call_target="tpu_custom_call" | custom-call | tf_op jit(solution)/shard_map/act/pallas_call | solution.py:28
  39.6 0.3 collective-permute-start.7
  39.9 1.0 %collective-permute-start.14 = (f32[32,512]{1,0:T(8,128)S(1)}, f32[32,512]{1,0:T(8,128)S(1)}, u32[]{:S(2)}, u32[]{:S(2)}) collective-permute-start(f32[32,512]{1,0:T(8,128)S(1)} %get-tuple-element.50), channel_id=1, source_target_pairs={{0,1},{1,0},{2,3},{3,2},{4,5},{5,4},{6,7},{7,6},{8,9},{9,8},{10,11... | collective-permute-start | bytes 196616 | tf_op jit(solution)/shard_map/ppermute | solution.py:382
  40.9 0.9 %collective-permute-done.14 = f32[32,512]{1,0:T(8,128)S(1)} collective-permute-done((f32[32,512]{1,0:T(8,128)S(1)}, f32[32,512]{1,0:T(8,128)S(1)}, u32[]{:S(2)}, u32[]{:S(2)}) %collective-permute-start.14) | collective-permute-done | bytes 65568 | tf_op jit(solution)/shard_map/ppermute | solution.py:382
  41.8 0.3 collective-permute-start.15
  42.1 3.2 %collective-permute-done.15 = f32[32,512]{1,0:T(8,128)S(1)} collective-permute-done((f32[32,512]{1,0:T(8,128)S(1)}, f32[32,512]{1,0:T(8,128)S(1)}, u32[]{:S(2)}, u32[]{:S(2)}) %collective-permute-start.15) | collective-permute-done | bytes 65568 | tf_op jit(solution)/shard_map/ppermute | solution.py:382
  45.3 1.2 %collective-permute-start.16 = (f32[32,512]{1,0:T(8,128)S(1)}, f32[32,512]{1,0:T(8,128)S(1)}, u32[]{:S(2)}, u32[]{:S(2)}) collective-permute-start(f32[32,512]{1,0:T(8,128)S(1)} %add.16), channel_id=1, source_target_pairs={{0,16},{16,0},{1,17},{17,1},{2,18},{18,2},{3,19},{19,3},{4,20},{20... | collective-permute-start | bytes 196616 | tf_op jit(solution)/shard_map/ppermute | solution.py:382
  46.5 7.4 %collective-permute-done.16 = f32[32,512]{1,0:T(8,128)S(1)} collective-permute-done((f32[32,512]{1,0:T(8,128)S(1)}, f32[32,512]{1,0:T(8,128)S(1)}, u32[]{:S(2)}, u32[]{:S(2)}) %collective-permute-start.16) | collective-permute-done | bytes 65568 | tf_op jit(solution)/shard_map/ppermute | solution.py:382
  53.9 0.3 collective-permute-start.17
  54.2 1.3 %collective-permute-start.8 = (f32[2,4,16,128]{3,2,1,0:T(8,128)S(1)}, f32[2,4,16,128]{3,2,1,0:T(8,128)S(1)}, u32[]{:S(2)}, u32[]{:S(2)}) collective-permute-start(f32[2,4,16,128]{3,2,1,0:T(8,128)S(1)} %get-tuple-element.43), channel_id=1, source_target_pairs={{0,4},{4,8},{8,12},{12,0},{1,5},{5,9},{9,13},{13,1},{2,6},{6,10},{... | collective-permute-start | bytes 196616 | tf_op jit(solution)/shard_map/ppermute | solution.py:118
  55.5 2.0 %collective-permute-start.9 = (f32[2,4,16,128]{3,2,1,0:T(8,128)S(1)}, f32[2,4,16,128]{3,2,1,0:T(8,128)S(1)}, u32[]{:S(2)}, u32[]{:S(2)}) collective-permute-start(f32[2,4,16,128]{3,2,1,0:T(8,128)S(1)} %get-tuple-element.44), channel_id=1, source_target_pairs={{4,0},{8,4},{12,8},{0,12},{5,1},{9,5},{13,9},{1,13},{6,2},{10,6},{... | collective-permute-start | bytes 196616 | tf_op jit(solution)/shard_map/ppermute | solution.py:119
  57.5 0.0 collective-permute-start.10
  57.5 0.0 collective-permute-done.17
  57.5 0.4 collective-permute-start.18
  57.9 0.1 slice_reduce_fusion.1
  58.0 5.2 %collective-permute-done.18 = f32[32,512]{1,0:T(8,128)S(1)} collective-permute-done((f32[32,512]{1,0:T(8,128)S(1)}, f32[32,512]{1,0:T(8,128)S(1)}, u32[]{:S(2)}, u32[]{:S(2)}) %collective-permute-start.18) | collective-permute-done | bytes 65568 | tf_op jit(solution)/shard_map/ppermute | solution.py:382
  63.2 2.7 %collective-permute-start.11 = (f32[2,2,16,128]{3,2,1,0:T(8,128)S(1)}, f32[2,2,16,128]{3,2,1,0:T(8,128)S(1)}, u32[]{:S(2)}, u32[]{:S(2)}) collective-permute-start(f32[2,2,16,128]{3,2,1,0:T(8,128)S(1)} %get-tuple-element.46), channel_id=1, source_target_pairs={{4,16},{8,20},{12,24},{0,28},{20,0},{24,4},{28,8},{16,12},{5,17},{... | collective-permute-start | bytes 98312 | tf_op jit(solution)/shard_map/ppermute | solution.py:112
  65.8 0.7 slice_reduce_fusion
  66.5 0.0 collective-permute-done.10.xy_low
  66.5 0.3 collective-permute-done.11.xy_high
  66.9 0.0 collective-permute-done.8.y_low
  66.9 0.0 collective-permute-done.9.y_high
  66.9 0.0 collective-permute-done.7.x_face
  66.9 0.5 pad_faces.3
  67.4 5.4 %collective-permute-start.12 = (f32[32,128]{1,0:T(8,128)S(1)}, f32[32,128]{1,0:T(8,128)S(1)}, u32[]{:S(2)}, u32[]{:S(2)}) collective-permute-start(f32[32,128]{1,0:T(8,128)S(1)} %get-tuple-element.48), channel_id=1, source_target_pairs={{0,1},{1,2},{2,3},{3,0},{4,5},{5,6},{6,7},{7,4},{8,9},{9,10},{10,1... | collective-permute-start | bytes 49160 | tf_op jit(solution)/shard_map/ppermute | solution.py:134
  72.8 0.0 collective-permute-start.13
  72.8 0.1 fusion.3
  72.9 0.2 reshape.33
  73.1 0.7 copy.18
  73.8 0.0 collective-permute-done.12.before
  73.8 2.2 %collective-permute-done.13.after = f32[32,128]{1,0:T(8,128)S(1)} collective-permute-done((f32[32,128]{1,0:T(8,128)S(1)}, f32[32,128]{1,0:T(8,128)S(1)}, u32[]{:S(2)}, u32[]{:S(2)}) %collective-permute-start.13) | collective-permute-done | bytes 16416 | tf_op jit(solution)/shard_map/ppermute | solution.py:135
  76.0 3.4 %grads.1 = f32[1024,128]{1,0:T(8,128)} custom-call(f32[2,112,16,128]{3,2,1,0:T(8,128)S(1)} %get-tuple-element.47.padded, f32[32,128]{1,0:T(8,128)S(1)} %collective-permute-done.12.before, f32[32,128]{1,0:T(8,128)S(1)} %collective-permute-done.13.after, f32[32,512]{1,0:T(8,128)S(1)} %add.19.sums, f32[16,128]{1,0:T(8,128)S(1)} %get-tuple-element.51.scales, ...), custom_call_target="tpu_custom_call" | custom-call | tf_op jit(solution)/shard_map/grads/pallas_call | solution.py:28
  (9 shorter events, 0.1 us)
Async XLA Ops:
  0.6 1.0 %copy-start.1 = (f32[16,4,16,128]{3,2,1,0:T(8,128)S(1)}, f32[16,4,16,128]{3,2,1,0:T(8,128)}, u32[]{:S(2)}) copy-start(f32[16,4,16,128]{3,2,1,0:T(8,128)} %param.5) | copy-start | bytes 1572868
  2.0 12.0 %collective-permute-start = (f32[2,1,16,16,128]{4,3,2,1,0:T(8,128)S(1)}, f32[2,1,16,16,128]{4,3,2,1,0:T(8,128)S(1)}, u32[]{:S(2)}, u32[]{:S(2)}) collective-permute-start(f32[2,1,16,16,128]{4,3,2,1,0:T(8,128)S(1)} %get-tuple-element.30), channel_id=1, source_target_pairs={{0,16},{16,0},{1,17},{17,1},{2,18},{18,2},{3,19},{19,3},{4,20},{20... | collective-permute-start | bytes 786440 | tf_op jit(solution)/shard_map/ppermute | solution.py:112
  4.1 9.9 %collective-permute-start.1 = (f32[1,4,16,128]{3,2,1,0:T(8,128)S(1)}, f32[1,4,16,128]{3,2,1,0:T(8,128)S(1)}, u32[]{:S(2)}, u32[]{:S(2)}) collective-permute-start(f32[1,4,16,128]{3,2,1,0:T(8,128)S(1)} %get-tuple-element.31), channel_id=1, source_target_pairs={{0,4},{4,8},{8,12},{12,0},{1,5},{5,9},{9,13},{13,1},{2,6},{6,10},{... | collective-permute-start | bytes 98312 | tf_op jit(solution)/shard_map/ppermute | solution.py:118
  5.4 8.6 %collective-permute-start.2 = (f32[1,4,16,128]{3,2,1,0:T(8,128)S(1)}, f32[1,4,16,128]{3,2,1,0:T(8,128)S(1)}, u32[]{:S(2)}, u32[]{:S(2)}) collective-permute-start(f32[1,4,16,128]{3,2,1,0:T(8,128)S(1)} %get-tuple-element.32), channel_id=1, source_target_pairs={{4,0},{8,4},{12,8},{0,12},{5,1},{9,5},{13,9},{1,13},{6,2},{10,6},{... | collective-permute-start | bytes 98312 | tf_op jit(solution)/shard_map/ppermute | solution.py:119
  7.4 6.5 %collective-permute-start.3 = (f32[2,1,16,128]{3,2,1,0:T(8,128)S(1)}, f32[2,1,16,128]{3,2,1,0:T(8,128)S(1)}, u32[]{:S(2)}, u32[]{:S(2)}) collective-permute-start(f32[2,1,16,128]{3,2,1,0:T(8,128)S(1)} %get-tuple-element.33), channel_id=1, source_target_pairs={{0,20},{4,24},{8,28},{12,16},{16,4},{20,8},{24,12},{28,0},{1,21},{... | collective-permute-start | bytes 49160 | tf_op jit(solution)/shard_map/ppermute | solution.py:112
  7.4 6.5 %collective-permute-start.4 = (f32[2,1,16,128]{3,2,1,0:T(8,128)S(1)}, f32[2,1,16,128]{3,2,1,0:T(8,128)S(1)}, u32[]{:S(2)}, u32[]{:S(2)}) collective-permute-start(f32[2,1,16,128]{3,2,1,0:T(8,128)S(1)} %get-tuple-element.34), channel_id=1, source_target_pairs={{4,16},{8,20},{12,24},{0,28},{20,0},{24,4},{28,8},{16,12},{5,17},{... | collective-permute-start | bytes 49160 | tf_op jit(solution)/shard_map/ppermute | solution.py:112
  11.6 23.2 %copy-start = (f32[16,4,16,128]{3,2,1,0:T(8,128)S(1)}, f32[16,4,16,128]{3,2,1,0:T(8,128)}, u32[]{:S(2)}) copy-start(f32[16,4,16,128]{3,2,1,0:T(8,128)} %param.9) | copy-start | bytes 1572868
  11.6 23.2 %copy-start.2 = (f32[16]{0:T(128)S(1)}, f32[16]{0:T(128)}, u32[]{:S(2)}) copy-start(f32[16]{0:T(128)} %param.7) | copy-start | bytes 196
  11.6 23.2 %copy-start.3 = (f32[16]{0:T(128)S(1)}, f32[16]{0:T(128)}, u32[]{:S(2)}) copy-start(f32[16]{0:T(128)} %param.8) | copy-start | bytes 196
  14.3 4.0 %collective-permute-start.5 = (f32[16,128]{1,0:T(8,128)S(1)}, f32[16,128]{1,0:T(8,128)S(1)}, u32[]{:S(2)}, u32[]{:S(2)}) collective-permute-start(f32[16,128]{1,0:T(8,128)S(1)} %get-tuple-element.36), channel_id=1, source_target_pairs={{0,1},{1,2},{2,3},{3,0},{4,5},{5,6},{6,7},{7,4},{8,9},{9,10},{10,1... | collective-permute-start | bytes 24584 | tf_op jit(solution)/shard_map/ppermute | solution.py:134
  17.5 3.1 %collective-permute-start.6 = (f32[16,128]{1,0:T(8,128)S(1)}, f32[16,128]{1,0:T(8,128)S(1)}, u32[]{:S(2)}, u32[]{:S(2)}) collective-permute-start(f32[16,128]{1,0:T(8,128)S(1)} %get-tuple-element.37), channel_id=1, source_target_pairs={{1,0},{2,1},{3,2},{0,3},{5,4},{6,5},{7,6},{4,7},{9,8},{10,9},{11,1... | collective-permute-start | bytes 24584 | tf_op jit(solution)/shard_map/ppermute | solution.py:135
  23.8 11.0 %all-to-all-start = ((f32[32,1,128]{2,1,0:T(1,128)}), f32[32,1,128]{2,1,0:T(1,128)S(1)}, u32[]{:S(2)}, u32[]{:S(2)}) async-start(f32[32,1,128]{2,1,0:T(1,128)} %bitcast.4), calls=%async_computation | async-start | bytes 32768 | tf_op jit(solution)/shard_map/all_to_all | solution.py:419
  39.6 27.3 %collective-permute-start.7 = (f32[2,2,16,16,128]{4,3,2,1,0:T(8,128)S(1)}, f32[2,2,16,16,128]{4,3,2,1,0:T(8,128)S(1)}, u32[]{:S(2)}, u32[]{:S(2)}) collective-permute-start(f32[2,2,16,16,128]{4,3,2,1,0:T(8,128)S(1)} %get-tuple-element.42), channel_id=1, source_target_pairs={{0,16},{16,0},{1,17},{17,1},{2,18},{18,2},{3,19},{19,3},{4,20},{20... | collective-permute-start | bytes 1572872 | tf_op jit(solution)/shard_map/ppermute | solution.py:112
  39.9 1.9 %collective-permute-start.14 = (f32[32,512]{1,0:T(8,128)S(1)}, f32[32,512]{1,0:T(8,128)S(1)}, u32[]{:S(2)}, u32[]{:S(2)}) collective-permute-start(f32[32,512]{1,0:T(8,128)S(1)} %get-tuple-element.50), channel_id=1, source_target_pairs={{0,1},{1,0},{2,3},{3,2},{4,5},{5,4},{6,7},{7,6},{8,9},{9,8},{10,11... | collective-permute-start | bytes 196616 | tf_op jit(solution)/shard_map/ppermute | solution.py:382
  41.8 3.5 %collective-permute-start.15 = (f32[32,512]{1,0:T(8,128)S(1)}, f32[32,512]{1,0:T(8,128)S(1)}, u32[]{:S(2)}, u32[]{:S(2)}) collective-permute-start(f32[32,512]{1,0:T(8,128)S(1)} %add.15), channel_id=1, source_target_pairs={{0,2},{1,3},{2,0},{3,1},{4,6},{5,7},{6,4},{7,5},{8,10},{9,11},{10,... | collective-permute-start | bytes 196616 | tf_op jit(solution)/shard_map/ppermute | solution.py:382
  45.3 8.6 %collective-permute-start.16 = (f32[32,512]{1,0:T(8,128)S(1)}, f32[32,512]{1,0:T(8,128)S(1)}, u32[]{:S(2)}, u32[]{:S(2)}) collective-permute-start(f32[32,512]{1,0:T(8,128)S(1)} %add.16), channel_id=1, source_target_pairs={{0,16},{16,0},{1,17},{17,1},{2,18},{18,2},{3,19},{19,3},{4,20},{20... | collective-permute-start | bytes 196616 | tf_op jit(solution)/shard_map/ppermute | solution.py:382
  53.9 3.5 %collective-permute-start.17 = (f32[32,512]{1,0:T(8,128)S(1)}, f32[32,512]{1,0:T(8,128)S(1)}, u32[]{:S(2)}, u32[]{:S(2)}) collective-permute-start(f32[32,512]{1,0:T(8,128)S(1)} %add.17), channel_id=1, source_target_pairs={{0,4},{4,0},{8,12},{12,8},{1,5},{5,1},{9,13},{13,9},{2,6},{6,2},{1... | collective-permute-start | bytes 196616 | tf_op jit(solution)/shard_map/ppermute | solution.py:382
  54.2 12.7 %collective-permute-start.8 = (f32[2,4,16,128]{3,2,1,0:T(8,128)S(1)}, f32[2,4,16,128]{3,2,1,0:T(8,128)S(1)}, u32[]{:S(2)}, u32[]{:S(2)}) collective-permute-start(f32[2,4,16,128]{3,2,1,0:T(8,128)S(1)} %get-tuple-element.43), channel_id=1, source_target_pairs={{0,4},{4,8},{8,12},{12,0},{1,5},{5,9},{9,13},{13,1},{2,6},{6,10},{... | collective-permute-start | bytes 196616 | tf_op jit(solution)/shard_map/ppermute | solution.py:118
  55.5 11.4 %collective-permute-start.9 = (f32[2,4,16,128]{3,2,1,0:T(8,128)S(1)}, f32[2,4,16,128]{3,2,1,0:T(8,128)S(1)}, u32[]{:S(2)}, u32[]{:S(2)}) collective-permute-start(f32[2,4,16,128]{3,2,1,0:T(8,128)S(1)} %get-tuple-element.44), channel_id=1, source_target_pairs={{4,0},{8,4},{12,8},{0,12},{5,1},{9,5},{13,9},{1,13},{6,2},{10,6},{... | collective-permute-start | bytes 196616 | tf_op jit(solution)/shard_map/ppermute | solution.py:119
  57.5 9.1 %collective-permute-start.10 = (f32[2,2,16,128]{3,2,1,0:T(8,128)S(1)}, f32[2,2,16,128]{3,2,1,0:T(8,128)S(1)}, u32[]{:S(2)}, u32[]{:S(2)}) collective-permute-start(f32[2,2,16,128]{3,2,1,0:T(8,128)S(1)} %get-tuple-element.45), channel_id=1, source_target_pairs={{0,20},{4,24},{8,28},{12,16},{16,4},{20,8},{24,12},{28,0},{1,21},{... | collective-permute-start | bytes 98312 | tf_op jit(solution)/shard_map/ppermute | solution.py:112
  57.5 5.7 %collective-permute-start.18 = (f32[32,512]{1,0:T(8,128)S(1)}, f32[32,512]{1,0:T(8,128)S(1)}, u32[]{:S(2)}, u32[]{:S(2)}) collective-permute-start(f32[32,512]{1,0:T(8,128)S(1)} %add.18), channel_id=1, source_target_pairs={{0,8},{4,12},{8,0},{12,4},{1,9},{5,13},{9,1},{13,5},{2,10},{6,14},... | collective-permute-start | bytes 196616 | tf_op jit(solution)/shard_map/ppermute | solution.py:382
  63.2 3.7 %collective-permute-start.11 = (f32[2,2,16,128]{3,2,1,0:T(8,128)S(1)}, f32[2,2,16,128]{3,2,1,0:T(8,128)S(1)}, u32[]{:S(2)}, u32[]{:S(2)}) collective-permute-start(f32[2,2,16,128]{3,2,1,0:T(8,128)S(1)} %get-tuple-element.46), channel_id=1, source_target_pairs={{4,16},{8,20},{12,24},{0,28},{20,0},{24,4},{28,8},{16,12},{5,17},{... | collective-permute-start | bytes 98312 | tf_op jit(solution)/shard_map/ppermute | solution.py:112
  67.4 6.4 %collective-permute-start.12 = (f32[32,128]{1,0:T(8,128)S(1)}, f32[32,128]{1,0:T(8,128)S(1)}, u32[]{:S(2)}, u32[]{:S(2)}) collective-permute-start(f32[32,128]{1,0:T(8,128)S(1)} %get-tuple-element.48), channel_id=1, source_target_pairs={{0,1},{1,2},{2,3},{3,0},{4,5},{5,6},{6,7},{7,4},{8,9},{9,10},{10,1... | collective-permute-start | bytes 49160 | tf_op jit(solution)/shard_map/ppermute | solution.py:134
  72.8 3.2 %collective-permute-start.13 = (f32[32,128]{1,0:T(8,128)S(1)}, f32[32,128]{1,0:T(8,128)S(1)}, u32[]{:S(2)}, u32[]{:S(2)}) collective-permute-start(f32[32,128]{1,0:T(8,128)S(1)} %get-tuple-element.49), channel_id=1, source_target_pairs={{1,0},{2,1},{3,2},{0,3},{5,4},{6,5},{7,6},{4,7},{9,8},{10,9},{11,1... | collective-permute-start | bytes 49160 | tf_op jit(solution)/shard_map/ppermute | solution.py:135
